TPU v7x, 32 devices: a whole 2x2x4 slice. The times are simulated.
32 devices in a mesh: blk: 8 (over y, x, core), tm: 4 (over z).
Axes of the slice: x: 2, y: 2, z: 4, core: 2. Of those that a mesh axis runs over, the one named last changes fastest.
Arguments:
- records: float32 [1024, 32768], P('blk', 'tm'), may hold values from -420 to 420
- gaps: int32 [2, 8, 8], P(None, 'blk', 'tm'), may hold values from 0 to 4096, as said below
Outputs:
- correlation: float32 [1024, 8, 4096], P(('blk', 'tm'))
Inputs may be any that keep to these rules, and one draw needn't show every extreme that they name: For every window, gaps[0] + gaps[1] <= 4096; a window either has no valid sample or at least 1024 of them. Among the 2 windows of one channel block on one index of tm, exactly one has valid samples.
All inputs are finite; a program needn't handle non-finite values.
Results may differ from a plain program's by a relative error of at most 0.0003.
Values sent between devices are 32-bit elements; how exact they have to be, the bound alone decides.
No kernel may reach another device: no remote copies, remote signals or barrier semaphores. Data moves between devices by JAX's collectives and lax.ppermute only.
A program may use at most 256 MiB of HBM per device.

v0:
```python
import functools
import math

import jax
import jax.numpy as jnp
import numpy as np
from jax import lax
from jax.experimental import pallas as pl
from jax.experimental.pallas import tpu as pltpu
from jax.sharding import PartitionSpec as P

NFFT = 4096
BAND = 64
EPS = 1e-05
LANES = 128
SUB = 8
RADIX = NFFT // LANES
HALF = RADIX // 2
ROWS = HALF + 1
QUART = LANES // 2
PAD = ROWS * SUB


def split_bf16(table):
    high = table.astype(jnp.bfloat16)
    low = (table - high.astype(np.float32)).astype(jnp.bfloat16)
    return high, low


def bin_order():
    half = np.arange(QUART // 2)
    return np.concatenate([2 * half, 2 * half + 1])


def dft_tables():
    spots = np.arange(LANES)[:, None]
    order = bin_order()[None, :]
    direct = 2.0 * np.pi / LANES * (spots * order % LANES)
    mirror = 2.0 * np.pi / LANES * (spots * (LANES - 1 - order) % LANES)
    upper = np.concatenate([np.cos(direct), np.cos(mirror), -np.sin(direct), np.sin(mirror)], 1)
    lower = np.concatenate([np.sin(direct), np.sin(mirror), np.cos(direct), -np.cos(mirror)], 1)
    full = np.concatenate([upper, lower], 0).astype(np.float32)
    tables = []
    for one in (full, full.T):
        high, low = split_bf16(one)
        tables.append(np.concatenate([high, high, low], 0))
    return tables


def twist_table():
    rows = np.arange(ROWS)[:, None]
    angle = 2.0 * np.pi / NFFT * (rows * np.arange(LANES)[None, :])
    return np.concatenate([np.cos(angle), np.sin(angle)], 0).astype(np.float32)


def bin_weights(norm):
    rows = np.arange(HALF)[:, None]
    order = bin_order()[None, :]
    direct = rows + RADIX * order
    mirror = np.where(rows == 0, HALF, RADIX - rows) + RADIX * order
    bins = np.concatenate([direct, mirror], 1)
    return (np.where(bins == 0, 1.0, 2.0) * np.where(bins % 2 == 0, 1.0, -1.0) * norm).astype(np.float32)


def turn(re, im, c, s):
    if abs(c - s) < 1e-12:
        return (re + im) * c, (im - re) * c
    if abs(c + s) < 1e-12:
        return (im - re) * s, -(re + im) * s
    return re * c + im * s, im * c - re * s


def real_fft(x):
    n = len(x)
    if n == 2:
        return [x[0] + x[1], x[0] - x[1]], [None, None]
    er, ei = real_fft(x[0::2])
    odr, odi = real_fft(x[1::2])
    half, quarter = n // 2, n // 4
    re, im = [None] * (half + 1), [None] * (half + 1)
    re[0], re[half] = er[0] + odr[0], er[0] - odr[0]
    re[quarter], im[quarter] = er[quarter], -odr[quarter]
    for k in range(1, quarter):
        angle = 2.0 * math.pi * k / n
        tr, ti = turn(odr[k], odi[k], math.cos(angle), math.sin(angle))
        re[k], im[k] = er[k] + tr, ei[k] + ti
        re[half - k], im[half - k] = er[k] - tr, ti - ei[k]
    return re, im


def real_fft_adjoint(re, im):
    half = len(re) - 1
    n = 2 * half
    if n == 2:
        return [re[0] + re[1], re[0] - re[1]]
    quarter = n // 4
    er, ei = [None] * (quarter + 1), [None] * (quarter + 1)
    odr, odi = [None] * (quarter + 1), [None] * (quarter + 1)
    er[0], odr[0] = re[0] + re[half], re[0] - re[half]
    er[quarter], odr[quarter] = re[quarter], -im[quarter]
    for k in range(1, quarter):
        er[k], ei[k] = re[k] + re[half - k], im[k] - im[half - k]
        tr, ti = re[k] - re[half - k], im[k] + im[half - k]
        angle = 2.0 * math.pi * k / n
        odr[k], odi[k] = turn(tr, ti, math.cos(angle), -math.sin(angle))
    even = real_fft_adjoint(er, ei)
    odd = real_fft_adjoint(odr, odi)
    out = [None] * n
    out[0::2] = even
    out[1::2] = odd
    return out


def matmul(rows, table):
    high = rows.astype(jnp.bfloat16)
    low = (rows - high.astype(jnp.float32)).astype(jnp.bfloat16)
    wide = jnp.concatenate([high, low, high], axis=1)
    return jnp.dot(wide, table, preferred_element_type=jnp.float32)


def lane_ids():
    return lax.broadcasted_iota(jnp.int32, (SUB, LANES), 1)


def lift(x, twist_ref, grid_ref, base):
    re, im = real_fft(x)
    for k in range(ROWS):
        if k == 0:
            zr, zi = re[0], jnp.zeros_like(re[0])
        else:
            c = twist_ref[k : k + 1, :]
            s = twist_ref[ROWS + k : ROWS + k + 1, :]
            if k == HALF:
                zr, zi = re[k] * c, -(re[k] * s)
            else:
                zr, zi = re[k] * c + im[k] * s, im[k] * c - re[k] * s
        spot = pl.ds(base + k * SUB, SUB)
        grid_ref[spot, :LANES] = zr
        grid_ref[spot, LANES:] = zi


def whiten(spec_ref, base):
    first = lane_ids() < QUART
    re, im = [], []
    for k in range(HALF):
        spot = pl.ds(base + k * SUB, SUB)
        r, i = spec_ref[spot, :LANES], spec_ref[spot, LANES:]
        if k == 0:
            last = pl.ds(base + HALF * SUB, SUB)
            r = jnp.where(first, r, spec_ref[last, :LANES])
            i = jnp.where(first, i, spec_ref[last, LANES:])
        re.append(r)
        im.append(i)
    power = re[0] * re[0] + im[0] * im[0]
    for r, i in zip(re[1:], im[1:]):
        power = power + (r * r + i * i)
    power = power + pltpu.roll(power, QUART, 1)
    power = power + pltpu.roll(power, QUART // 2, 1)
    scale = 1.0 / jnp.sqrt(power * (1.0 / BAND) + EPS)
    return [r * scale for r in re], [i * scale for i in im]


def source_kernel(windows, group, me_ref, raw_ref, twist_ref, table_ref, weight_ref, out_ref, grid_ref):
    sources = raw_ref.shape[0] // (windows * RADIX)
    lanes = lane_ids()
    me = me_ref[0]
    span = windows * RADIX
    for w in range(windows):
        own = jnp.broadcast_to(raw_ref[pl.ds(me * span + w * RADIX, 1), :1], (SUB, 1))
        for g in range(sources // group):
            x = [raw_ref[pl.ds(g * group * span + w * RADIX + v, SUB, stride=span), :] for v in range(RADIX)]
            match = jnp.where(x[0][:, :1] == own, 1.0, 0.0)
            x[0] = jnp.where(lanes == 0, 0.0, x[0])
            lift(x, twist_ref, grid_ref, 0)
            grid_ref[...] = matmul(grid_ref[...], table_ref[...])
            re, im = whiten(grid_ref, 0)
            for k in range(HALF):
                weight = weight_ref[k : k + 1, :] * match
                spot = pl.ds((w * HALF + k) * sources + g * group, SUB)
                out_ref[spot, :LANES] = re[k] * weight
                out_ref[spot, LANES:] = im[k] * weight


def main_kernel(windows, batch, *refs):
    ins, (source_ref, twist_ref, table_ref, back_ref, out_ref, grid_ref, spec_ref, cross_ref) = refs[:windows], refs[windows:]
    group = pl.program_id(1)
    sources = source_ref.shape[0] // (windows * HALF)
    first = lane_ids() < QUART

    @pl.when(group == 0)
    def _():
        for w in range(windows):
            x = [ins[w][:, v * LANES : (v + 1) * LANES] for v in range(RADIX)]
            lift(x, twist_ref, grid_ref, w * PAD)
        grid_ref[...] = matmul(grid_ref[...], table_ref[...])
        for w in range(windows):
            re, im = whiten(grid_ref, w * PAD)
            for k in range(HALF):
                spec_ref[:, w * HALF + k, :LANES] = re[k]
                spec_ref[:, w * HALF + k, LANES:] = im[k]

    def some(step, _):
        start = step * batch

        def combine(k):
            found = []
            parts = []
            for w in range(windows):
                spot = pl.ds((w * HALF + k) * sources + group * SUB, SUB)
                parts.append((source_ref[spot, :LANES], source_ref[spot, LANES:]))
            for c in range(batch):
                re = im = None
                for w in range(windows):
                    ur, ui = parts[w]
                    row = w * HALF + k
                    sr = spec_ref[start + c, row : row + 1, :LANES]
                    si = spec_ref[start + c, row : row + 1, LANES:]
                    r, i = sr * ur + si * ui, si * ur - sr * ui
                    re, im = (r, i) if re is None else (re + r, im + i)
                found.append((re, im))
            return found

        for c, (re, im) in enumerate(combine(0)):
            cross_ref[pl.ds(c * PAD, SUB), :LANES] = jnp.where(first, re, 0.0)
            cross_ref[pl.ds(c * PAD, SUB), LANES:] = jnp.where(first, im, 0.0)
            cross_ref[pl.ds(c * PAD + HALF * SUB, SUB), :LANES] = jnp.where(first, 0.0, re)
            cross_ref[pl.ds(c * PAD + HALF * SUB, SUB), LANES:] = jnp.where(first, 0.0, im)
        for k in range(1, HALF):
            for c, (re, im) in enumerate(combine(k)):
                spot = pl.ds(c * PAD + k * SUB, SUB)
                cross_ref[spot, :LANES] = re
                cross_ref[spot, LANES:] = im
        cross_ref[...] = matmul(cross_ref[...], back_ref[...])
        for c in range(batch):
            re, im = [], []
            for k in range(ROWS):
                spot = pl.ds(c * PAD + k * SUB, SUB)
                r, i = cross_ref[spot, :LANES], cross_ref[spot, LANES:]
                if k == 0:
                    i = None
                else:
                    cos = twist_ref[k : k + 1, :]
                    sin = twist_ref[ROWS + k : ROWS + k + 1, :]
                    r, i = r * cos - i * sin, (None if k == HALF else i * cos + r * sin)
                re.append(r)
                im.append(i)
            lags = real_fft_adjoint(re, im)
            for v in range(RADIX):
                out_ref[start + c, :, v * LANES : (v + 1) * LANES] = lags[v]
        return 0

    lax.fori_loop(0, SUB // batch, some, 0)


def resident(array):
    return pl.BlockSpec(array.shape, lambda *_: (0,) * array.ndim)


def source_spectra(raw, me, windows, tables):
    twist, forward, _, weights = tables
    sources = raw.shape[0] // (windows * RADIX)
    group = SUB
    shape = (windows * HALF * sources, 2 * LANES)
    return pl.pallas_call(
        functools.partial(source_kernel, windows, group),
        out_shape=jax.ShapeDtypeStruct(shape, jnp.float32),
        grid_spec=pltpu.PrefetchScalarGridSpec(
            num_scalar_prefetch=1,
            grid=(1,),
            in_specs=[resident(raw), resident(twist), resident(forward), resident(weights)],
            out_specs=pl.BlockSpec(shape, lambda *_: (0, 0)),
            scratch_shapes=[pltpu.VMEM((PAD, 2 * LANES), jnp.float32)],
        ),
        name="sources",
    )(me.reshape(1), raw, twist, forward, weights)


def correlations(pieces, source, tables, total, first, before, batch=4):
    twist, forward, back, _ = tables
    windows = len(pieces)
    sources = source.shape[0] // (windows * HALF)
    rows = pieces[0].shape[0]
    offset = first // SUB
    args = [*pieces, source, twist, forward, back]
    specs = [pl.BlockSpec((SUB, NFFT), lambda c, g: (c, 0))] * windows
    specs += [resident(a) for a in args[windows:]]
    aliases = {}
    if before is not None:
        aliases = {len(args): 0}
        args.append(before)
        specs.append(pl.BlockSpec(memory_space=pl.ANY))

    def body(*refs):
        if before is not None:
            refs = refs[: windows + 4] + refs[windows + 5 :]
        main_kernel(windows, batch, *refs)

    return pl.pallas_call(
        body,
        out_shape=jax.ShapeDtypeStruct((total, sources, NFFT), jnp.float32),
        grid=(rows // SUB, sources // SUB),
        in_specs=specs,
        out_specs=pl.BlockSpec((SUB, SUB, NFFT), lambda c, g: (c + offset, g, 0)),
        scratch_shapes=[
            pltpu.VMEM((windows * PAD, 2 * LANES), jnp.float32),
            pltpu.VMEM((SUB, windows * HALF, 2 * LANES), jnp.float32),
            pltpu.VMEM((batch * PAD, 2 * LANES), jnp.float32),
        ],
        input_output_aliases=aliases,
        compiler_params=pltpu.CompilerParams(vmem_limit_bytes=40 * 2**20),
        name=f"lags_{first}",
    )(*args)


def shards(records, gaps):
    width = records.shape[0]
    slots = records.shape[1] // NFFT
    windows = lax.axis_size("tm")
    here = lax.axis_index("tm")
    mine = width // windows
    starts, counts = gaps[0, 0], gaps[1, 0]
    live = jnp.argmax(counts).astype(jnp.int32)
    start, count = starts[live], counts[live]
    spots = np.arange(NFFT)
    taper = jnp.asarray((0.5 - 0.5 * np.cos(2.0 * np.pi / NFFT * spots)).astype(np.float32))
    taper = jnp.where((spots >= start) & (spots < start + count), taper, 0.0)
    frames = lax.dynamic_slice(records, (jnp.int32(0), live * NFFT), (width, NFFT))
    tapered = jnp.where(taper == 0.0, 0.0, frames) * taper
    parted = tapered.reshape(windows, mine, NFFT)

    def shift(array, step):
        pairs = [(i, (i + step) % windows) for i in range(windows)]
        return lax.ppermute(array, "tm", pairs)

    def part(step):
        return lax.dynamic_index_in_dim(parted, (here + step) % windows, 0, keepdims=False)

    last = SUB
    cut = mine - last
    steps = list(range(1, windows))
    own = part(0)
    head = [own[:cut]] + [shift(part(d)[:cut], d) for d in steps]
    tail = [own[cut:]] + [shift(part(d)[cut:], d) for d in steps]

    row = jnp.where(spots == 0, live.astype(jnp.float32), tapered[0]).reshape(RADIX, LANES)
    rows = jnp.stack([row] + [shift(row, d) for d in steps])
    raw = lax.all_gather(rows, "blk", axis=0, tiled=False)
    raw = raw.reshape(-1, LANES)

    norm = 1.0 / math.sqrt(NFFT * slots * windows)
    forward, back = dft_tables()
    tables = (jnp.asarray(twist_table()), jnp.asarray(forward), jnp.asarray(back), jnp.asarray(bin_weights(norm)))
    source = source_spectra(raw, lax.axis_index("blk").astype(jnp.int32), windows, tables)
    out = correlations(head, source, tables, mine, 0, None)
    return correlations(tail, source, tables, mine, cut, out)


def solution(mesh):
    in_specs = (P("blk", "tm"), P(None, "blk", "tm"))
    out_specs = P(("blk", "tm"), None, None)
    return jax.shard_map(shards, mesh=mesh, in_specs=in_specs, out_specs=out_specs, check_vma=False)
```

profile of v0, /device:TPU:0, one launch (start us, length us, event | category | flops | bytes accessed | tf_op | source)
XLA Modules:
  0.0 76.7 jit_solution(10385632763530839251)
XLA Ops:
  0.0 0.7 fusion.2
  0.7 1.4 %bitcast_reduce_fusion = (s32[]{:T(128)}, s32[]{:T(128)}) fusion(s32[2,1,2]{2,1,0:T(1,128)} %param.10), kind=kLoop, calls=%fused_computation.18 | loop fusion | flops 7 | bytes 16 | tf_op jit(solution)/shard_map/shards/reduce | solution.py:322
  4.8 0.6 constant_dynamic-slice_fusion
  6.7 1.4 %broadcast_compare_fusion = pred[4096]{0:T(1024)(128)(4,1)S(1)} fusion(f32[4096]{0:T(1024)} %constant.90.clone, s32[]{:T(128)S(6)} %add.55, s32[]{:T(128)} %bitcast.1), kind=kLoop, calls=%fused_computation.15 | loop fusion | flops 20480 | bytes 20488 | tf_op jit(solution)/shard_map/eq | solution.py:328
  8.0 1.3 %fusion.1 = f32[4096]{0:T(1024)S(1)} fusion(f32[4096]{0:T(1024)} %constant.90.clone, s32[]{:T(128)S(6)} %add.55, s32[]{:T(128)} %bitcast.1), kind=kLoop, calls=%fused_computation.14 | loop fusion | flops 16384 | bytes 32776 | tf_op jit(solution)/shard_map/jit(_where)/select_n | solution.py:326
  10.1 0.0 copy-start.5
  10.1 1.8 %select_multiply_fusion = f32[128,4096]{1,0:T(8,128)S(1)} fusion(f32[128,8192]{1,0:T(8,128)} %param.9, s32[]{:T(128)S(6)} %select_n.66, f32[4096]{0:T(1024)S(1)} %fusion.1, pred[4096]{0:T(1024)(128)(4,1)S(1)} %broadcast_compare_fusion), kind=kLoop, calls=%fused_computation | loop fusion | flops 1048576 | bytes 4214788 | tf_op jit(solution)/shard_map/mul | solution.py:328
  11.9 0.0 copy-done.5
  11.9 0.0 copy-start.4
  12.0 5.1 %collective-permute-start.5 = (f32[32,128]{1,0:T(8,128)S(1)}, f32[32,128]{1,0:T(8,128)S(1)}, u32[]{:S(2)}, u32[]{:S(2)}) collective-permute-start(f32[32,128]{1,0:T(8,128)S(1)} %bitcast.31), channel_id=1, source_target_pairs={{0,3},{1,0},{2,1},{3,2},{4,7},{5,4},{6,5},{7,6},{8,11},{9,8},{10,9... | collective-permute-start | bytes 49160 | tf_op jit(solution)/shard_map/ppermute | solution.py:333
  17.1 0.0 collective-permute-start.4
  17.1 1.0 %collective-permute-start.3 = (f32[32,128]{1,0:T(8,128)S(1)}, f32[32,128]{1,0:T(8,128)S(1)}, u32[]{:S(2)}, u32[]{:S(2)}) collective-permute-start(f32[32,128]{1,0:T(8,128)S(1)} %bitcast.33), channel_id=1, source_target_pairs={{0,1},{1,2},{2,3},{3,0},{4,5},{5,6},{6,7},{7,4},{8,9},{9,10},{10,1... | collective-permute-start | bytes 49160 | tf_op jit(solution)/shard_map/ppermute | solution.py:333
  18.1 1.0 %dynamic-slice_bitcast_fusion = (f32[24,4096]{1,0:T(8,128)}, f32[24,4096]{1,0:T(8,128)}, f32[24,4096]{1,0:T(8,128)}, f32[24,4096]{1,0:T(8,128)S(1)}) fusion(f32[4,32,4096]{2,1,0:T(8,128)S(1)} %bitcast.28, s32[]{:T(128)S(6)} %select_n.75, s32[]{:T(128)S(6)} %select_n.73, s32[]{:T(128)S(6)} %select_n.71, s32[]{:T(128)S(6)} %select_n.69), kind=kLoop, calls=%fused_computation.1 | loop fusion | bytes 3145744 | tf_op jit(solution)/shard_map/slice | solution.py:342
  19.1 0.0 copy-done.4
  19.1 0.0 copy-start.1
  19.1 0.0 copy-start.2
  19.1 0.0 copy-start.3
  19.1 2.9 %collective-permute-start.8 = (f32[24,4096]{1,0:T(8,128)}, f32[24,4096]{1,0:T(8,128)S(1)}, u32[]{:S(2)}, u32[]{:S(2)}) collective-permute-start(f32[24,4096]{1,0:T(8,128)} %get-tuple-element.7), channel_id=1, source_target_pairs={{0,3},{1,0},{2,1},{3,2},{4,7},{5,4},{6,5},{7,6},{8,11},{9,8},{10,9... | collective-permute-start | bytes 1179656 | tf_op jit(solution)/shard_map/ppermute | solution.py:333
  22.0 1.1 %collective-permute-start.7 = (f32[24,4096]{1,0:T(8,128)}, f32[24,4096]{1,0:T(8,128)S(1)}, u32[]{:S(2)}, u32[]{:S(2)}) collective-permute-start(f32[24,4096]{1,0:T(8,128)} %get-tuple-element.8), channel_id=1, source_target_pairs={{0,2},{1,3},{2,0},{3,1},{4,6},{5,7},{6,4},{7,5},{8,10},{9,11},{10,... | collective-permute-start | bytes 1179656 | tf_op jit(solution)/shard_map/ppermute | solution.py:333
  23.1 0.0 collective-permute-done.5
  23.1 0.0 collective-permute-start.6
  23.1 1.1 %dynamic-slice_bitcast_fusion.4 = (f32[8,4096]{1,0:T(8,128)S(1)}, f32[8,4096]{1,0:T(8,128)S(1)}, f32[8,4096]{1,0:T(8,128)S(1)}, f32[8,4096]{1,0:T(8,128)S(1)}) fusion(f32[4,32,4096]{2,1,0:T(8,128)} %bitcast.29, s32[]{:T(128)S(6)} %select_n.75, s32[]{:T(128)S(6)} %add.68, s32[]{:T(128)S(6)} %select_n.73, s32[]{:T(128)S(6)} %select_n.71, s32[]{:T(128)S(6)} %select_n.69), kind=kLoop, calls=%fused_computation.5 | loop fusion | bytes 1048596 | tf_op jit(solution)/shard_map/slice | solution.py:343
  24.3 0.0 collective-permute-done.4
  24.3 3.9 %collective-permute-start.2 = (f32[8,4096]{1,0:T(8,128)S(1)}, f32[8,4096]{1,0:T(8,128)S(1)}, u32[]{:S(2)}, u32[]{:S(2)}) collective-permute-start(f32[8,4096]{1,0:T(8,128)S(1)} %get-tuple-element.11), channel_id=1, source_target_pairs={{0,3},{1,0},{2,1},{3,2},{4,7},{5,4},{6,5},{7,6},{8,11},{9,8},{10,9... | collective-permute-start | bytes 393224 | tf_op jit(solution)/shard_map/ppermute | solution.py:333
  28.1 0.0 collective-permute-done.3
  28.1 0.0 collective-permute-start.1
  28.2 4.4 %collective-permute-done.8.refs_3_ = f32[24,4096]{1,0:T(8,128)S(1)} collective-permute-done((f32[24,4096]{1,0:T(8,128)}, f32[24,4096]{1,0:T(8,128)S(1)}, u32[]{:S(2)}, u32[]{:S(2)}) %collective-permute-start.8) | collective-permute-done | bytes 393248 | tf_op jit(solution)/shard_map/ppermute | solution.py:333
  32.5 19.5 %collective-permute-start = (f32[8,4096]{1,0:T(8,128)S(1)}, f32[8,4096]{1,0:T(8,128)S(1)}, u32[]{:S(2)}, u32[]{:S(2)}) collective-permute-start(f32[8,4096]{1,0:T(8,128)S(1)} %get-tuple-element.13), channel_id=1, source_target_pairs={{0,1},{1,2},{2,3},{3,0},{4,5},{5,6},{6,7},{7,4},{8,9},{9,10},{10,1... | collective-permute-start | bytes 393224 | tf_op jit(solution)/shard_map/ppermute | solution.py:333
  52.0 10.9 %all-gather = f32[32,32,128]{2,1,0:T(8,128)} all-gather(f32[4,32,128]{2,1,0:T(8,128)S(1)} %pad_maximum_fusion), channel_id=2, replica_groups=mesh['blk'=8,'tm'=4] {'blk'}, dimensions={0}, use_global_device_ids=true | all-gather | bytes 589824 | tf_op jit(solution)/shard_map/all_gather | solution.py:347
  62.9 2.9 %sources.1.refs_4_ = f32[512,256]{1,0:T(8,128)} custom-call(s32[1]{0:T(128)} %bitcast.8.me_ref, f32[1024,128]{1,0:T(8,128)} %bitcast.30, f32[34,128]{1,0:T(8,128)} %constant.92.clone.twist_ref.refs_5_, bf16[768,256]{1,0:T(8,128)(2,1)} %constant.93.clone.table_ref.refs_6_, f32[16,128]{1,0:T(8,128)} %constant.95.clone.weight_ref), custom_call_target="tpu_custom_call" | custom-call | tf_op jit(solution)/shard_map/sources/pallas_call | solution.py:264
  65.8 0.0 collective-permute-done.7.refs_2_
  65.8 0.0 collective-permute-done.6.refs_1_
  65.8 0.0 copy-done.1
  65.8 0.0 copy-done.2
  65.8 0.0 copy-done.3
  65.8 0.0 copy-start
  65.9 1.0 %copy-done = f32[512,256]{1,0:T(8,128)S(1)} copy-done((f32[512,256]{1,0:T(8,128)S(1)}, f32[512,256]{1,0:T(8,128)}, u32[]{:S(2)}) %copy-start) | copy-done | bytes 524312
  66.9 6.9 %lags_0.1.refs_8_ = f32[32,8,4096]{2,1,0:T(8,128)} custom-call(f32[24,4096]{1,0:T(8,128)S(1)} %get-tuple-element.10.refs_0_, f32[24,4096]{1,0:T(8,128)S(1)} %collective-permute-done.6.refs_1_, f32[24,4096]{1,0:T(8,128)S(1)} %collective-permute-done.7.refs_2_, f32[24,4096]{1,0:T(8,128)S(1)} %collective-permute-done.8.refs_3_, f32[512,256]{1,0:T(8,128)S(1)} %copy-done, ...), custom_call_target="tpu_custom_call" | custom-call | tf_op jit(solution)/shard_map/lags_0/pallas_call | solution.py:298
  73.8 0.0 collective-permute-done.2.refs_3_
  73.8 0.0 collective-permute-done.1.refs_2_
  73.8 0.0 collective-permute-done.refs_1_
  73.8 2.9 %lags_24.1 = f32[32,8,4096]{2,1,0:T(8,128)} custom-call(f32[8,4096]{1,0:T(8,128)S(1)} %get-tuple-element.14.refs_0_, f32[8,4096]{1,0:T(8,128)S(1)} %collective-permute-done.refs_1_, f32[8,4096]{1,0:T(8,128)S(1)} %collective-permute-done.1.refs_2_, f32[8,4096]{1,0:T(8,128)S(1)} %collective-permute-done.2.refs_3_, ...), custom_call_target="tpu_custom_call", output_to_operand_aliasing={{}: (8, {})} | custom-call | tf_op jit(solution)/shard_map/lags_24/pallas_call | solution.py:298
  (2 shorter events, 0.0 us)
Async XLA Ops:
  10.1 1.8 %copy-start.5 = (pred[1,4096]{1,0:T(4,128)(4,1)S(1)}, pred[1,4096]{1,0:T(4,128)(4,1)}, u32[]{:S(2)}) copy-start(pred[1,4096]{1,0:T(4,128)(4,1)} %constant.97) | copy-start | bytes 12292
  11.9 7.2 %copy-start.4 = (f32[128,4096]{1,0:T(8,128)}, f32[128,4096]{1,0:T(8,128)S(1)}, u32[]{:S(2)}) copy-start(f32[128,4096]{1,0:T(8,128)S(1)} %select_multiply_fusion) | copy-start | bytes 6291460
  12.0 11.2 %collective-permute-start.5 = (f32[32,128]{1,0:T(8,128)S(1)}, f32[32,128]{1,0:T(8,128)S(1)}, u32[]{:S(2)}, u32[]{:S(2)}) collective-permute-start(f32[32,128]{1,0:T(8,128)S(1)} %bitcast.31), channel_id=1, source_target_pairs={{0,3},{1,0},{2,1},{3,2},{4,7},{5,4},{6,5},{7,6},{8,11},{9,8},{10,9... | collective-permute-start | bytes 49160 | tf_op jit(solution)/shard_map/ppermute | solution.py:333
  17.1 7.2 %collective-permute-start.4 = (f32[32,128]{1,0:T(8,128)S(1)}, f32[32,128]{1,0:T(8,128)S(1)}, u32[]{:S(2)}, u32[]{:S(2)}) collective-permute-start(f32[32,128]{1,0:T(8,128)S(1)} %bitcast.32), channel_id=1, source_target_pairs={{0,2},{1,3},{2,0},{3,1},{4,6},{5,7},{6,4},{7,5},{8,10},{9,11},{10,... | collective-permute-start | bytes 49160 | tf_op jit(solution)/shard_map/ppermute | solution.py:333
  17.1 11.1 %collective-permute-start.3 = (f32[32,128]{1,0:T(8,128)S(1)}, f32[32,128]{1,0:T(8,128)S(1)}, u32[]{:S(2)}, u32[]{:S(2)}) collective-permute-start(f32[32,128]{1,0:T(8,128)S(1)} %bitcast.33), channel_id=1, source_target_pairs={{0,1},{1,2},{2,3},{3,0},{4,5},{5,6},{6,7},{7,4},{8,9},{9,10},{10,1... | collective-permute-start | bytes 49160 | tf_op jit(solution)/shard_map/ppermute | solution.py:333
  19.1 46.7 %copy-start.1 = (bf16[768,256]{1,0:T(8,128)(2,1)S(1)}, bf16[768,256]{1,0:T(8,128)(2,1)}, u32[]{:S(2)}) copy-start(bf16[768,256]{1,0:T(8,128)(2,1)} %constant.93.clone.table_ref.refs_6_) | copy-start | bytes 1179652
  19.1 46.7 %copy-start.2 = (bf16[768,256]{1,0:T(8,128)(2,1)S(1)}, bf16[768,256]{1,0:T(8,128)(2,1)}, u32[]{:S(2)}) copy-start(bf16[768,256]{1,0:T(8,128)(2,1)} %constant.94.clone.refs_7_) | copy-start | bytes 1179652
  19.1 46.7 %copy-start.3 = (f32[34,128]{1,0:T(8,128)S(1)}, f32[34,128]{1,0:T(8,128)}, u32[]{:S(2)}) copy-start(f32[34,128]{1,0:T(8,128)} %constant.92.clone.twist_ref.refs_5_) | copy-start | bytes 52228
  19.1 13.4 %collective-permute-start.8 = (f32[24,4096]{1,0:T(8,128)}, f32[24,4096]{1,0:T(8,128)S(1)}, u32[]{:S(2)}, u32[]{:S(2)}) collective-permute-start(f32[24,4096]{1,0:T(8,128)} %get-tuple-element.7), channel_id=1, source_target_pairs={{0,3},{1,0},{2,1},{3,2},{4,7},{5,4},{6,5},{7,6},{8,11},{9,8},{10,9... | collective-permute-start | bytes 1179656 | tf_op jit(solution)/shard_map/ppermute | solution.py:333
  22.0 43.8 %collective-permute-start.7 = (f32[24,4096]{1,0:T(8,128)}, f32[24,4096]{1,0:T(8,128)S(1)}, u32[]{:S(2)}, u32[]{:S(2)}) collective-permute-start(f32[24,4096]{1,0:T(8,128)} %get-tuple-element.8), channel_id=1, source_target_pairs={{0,2},{1,3},{2,0},{3,1},{4,6},{5,7},{6,4},{7,5},{8,10},{9,11},{10,... | collective-permute-start | bytes 1179656 | tf_op jit(solution)/shard_map/ppermute | solution.py:333
  23.1 42.7 %collective-permute-start.6 = (f32[24,4096]{1,0:T(8,128)}, f32[24,4096]{1,0:T(8,128)S(1)}, u32[]{:S(2)}, u32[]{:S(2)}) collective-permute-start(f32[24,4096]{1,0:T(8,128)} %get-tuple-element.9), channel_id=1, source_target_pairs={{0,1},{1,2},{2,3},{3,0},{4,5},{5,6},{6,7},{7,4},{8,9},{9,10},{10,1... | collective-permute-start | bytes 1179656 | tf_op jit(solution)/shard_map/ppermute | solution.py:333
  24.3 49.5 %collective-permute-start.2 = (f32[8,4096]{1,0:T(8,128)S(1)}, f32[8,4096]{1,0:T(8,128)S(1)}, u32[]{:S(2)}, u32[]{:S(2)}) collective-permute-start(f32[8,4096]{1,0:T(8,128)S(1)} %get-tuple-element.11), channel_id=1, source_target_pairs={{0,3},{1,0},{2,1},{3,2},{4,7},{5,4},{6,5},{7,6},{8,11},{9,8},{10,9... | collective-permute-start | bytes 393224 | tf_op jit(solution)/shard_map/ppermute | solution.py:333
  28.1 45.6 %collective-permute-start.1 = (f32[8,4096]{1,0:T(8,128)S(1)}, f32[8,4096]{1,0:T(8,128)S(1)}, u32[]{:S(2)}, u32[]{:S(2)}) collective-permute-start(f32[8,4096]{1,0:T(8,128)S(1)} %get-tuple-element.12), channel_id=1, source_target_pairs={{0,2},{1,3},{2,0},{3,1},{4,6},{5,7},{6,4},{7,5},{8,10},{9,11},{10,... | collective-permute-start | bytes 393224 | tf_op jit(solution)/shard_map/ppermute | solution.py:333
  32.5 41.3 %collective-permute-start = (f32[8,4096]{1,0:T(8,128)S(1)}, f32[8,4096]{1,0:T(8,128)S(1)}, u32[]{:S(2)}, u32[]{:S(2)}) collective-permute-start(f32[8,4096]{1,0:T(8,128)S(1)} %get-tuple-element.13), channel_id=1, source_target_pairs={{0,1},{1,2},{2,3},{3,0},{4,5},{5,6},{6,7},{7,4},{8,9},{9,10},{10,1... | collective-permute-start | bytes 393224 | tf_op jit(solution)/shard_map/ppermute | solution.py:333
  65.8 1.0 %copy-start = (f32[512,256]{1,0:T(8,128)S(1)}, f32[512,256]{1,0:T(8,128)}, u32[]{:S(2)}) copy-start(f32[512,256]{1,0:T(8,128)} %sources.1.refs_4_) | copy-start | bytes 1572868
where the time goes:
time: 77.2 us; the launch traced here: 76.7 us
  starting transfers between devices  33.5 us (43%)
  Pallas kernels  12.7 us (16%)
  blocking collectives  10.9 us (14%)
  other arithmetic  5.91 us (8%)
  between operations  4.8 us (6%)
  local copies, waits for them, and re-layouts  4.53 us (6%)
  waiting for transfers between devices  4.4 us (6%)
    ppermute x9, starting transfers between devices, shift(): return lax.ppermute(array, 'tm', pairs)  33.5 us
    all_gather x1, blocking collectives, shards(): raw = lax.all_gather(rows, 'blk', axis=0, tiled=False)  10.9 us
    pallas_call x2, Pallas kernels, correlations(): pl.pallas_call(body, out_shape=jax.ShapeDtypeStruct((total, sources, NFFT...  9.84 us
    ppermute x9, waiting for transfers between devices, shift(): return lax.ppermute(array, 'tm', pairs)  4.4 us
    pallas_call x1, Pallas kernels, source_spectra(): pl.pallas_call(functools.partial(source_kernel, windows, group), out_shap...  2.88 us
    mul x1, other arithmetic, shards(): tapered = jnp.where(taper == 0.0, 0.0, frames) * taper  1.8 us
  transfers between devices with their start and end apart: 9, of which 1 were waited for; matrix products, arithmetic and copies ran while one was open for 3% of the time, Pallas kernels for 13%

commit v1 on v0

--- a/solution.py
+++ b/solution.py
@@ -181,8 +181,10 @@
                 out_ref[spot, LANES:] = im[k] * weight
 
 
-def main_kernel(windows, batch, *refs):
-    ins, (source_ref, twist_ref, table_ref, back_ref, out_ref, grid_ref, spec_ref, cross_ref) = refs[:windows], refs[windows:]
+def main_kernel(windows, batch, split, *refs):
+    ins, refs = refs[:windows], refs[windows:]
+    extra, refs = (refs[0], refs[1:]) if split is not None else (None, refs)
+    source_ref, twist_ref, table_ref, back_ref, out_ref, grid_ref, spec_ref, cross_ref = refs
     group = pl.program_id(1)
     sources = source_ref.shape[0] // (windows * HALF)
     first = lane_ids() < QUART
@@ -191,6 +193,9 @@
     def _():
         for w in range(windows):
             x = [ins[w][:, v * LANES : (v + 1) * LANES] for v in range(RADIX)]
+            if w == split:
+                lead = pl.program_id(0) == 0
+                x = [jnp.where(lead, extra[1:, v, :], x[v]) for v in range(RADIX)]
             lift(x, twist_ref, grid_ref, w * PAD)
         grid_ref[...] = matmul(grid_ref[...], table_ref[...])
         for w in range(windows):
@@ -275,25 +280,33 @@
     )(me.reshape(1), raw, twist, forward, weights)
 
 
-def correlations(pieces, source, tables, total, first, before, batch=4):
+def correlations(pieces, starts, lead, source, tables, total, first, rows, before, batch=4):
     twist, forward, back, _ = tables
     windows = len(pieces)
     sources = source.shape[0] // (windows * HALF)
-    rows = pieces[0].shape[0]
     offset = first // SUB
-    args = [*pieces, source, twist, forward, back]
-    specs = [pl.BlockSpec((SUB, NFFT), lambda c, g: (c, 0))] * windows
-    specs += [resident(a) for a in args[windows:]]
+    args = list(pieces)
+    shifts = [(first - s) // SUB for s in starts]
+    specs = [pl.BlockSpec((SUB, NFFT), lambda c, g, n=n: (jnp.maximum(c + n, 0), 0)) for n in shifts]
+    split = None
+    if lead is not None:
+        split = starts.index(SUB)
+        args.append(lead)
+        specs.append(resident(lead))
+    fixed = [source, twist, forward, back]
+    args += fixed
+    specs += [resident(a) for a in fixed]
+    inputs = len(args)
     aliases = {}
     if before is not None:
-        aliases = {len(args): 0}
+        aliases = {inputs: 0}
         args.append(before)
         specs.append(pl.BlockSpec(memory_space=pl.ANY))
 
     def body(*refs):
         if before is not None:
-            refs = refs[: windows + 4] + refs[windows + 5 :]
-        main_kernel(windows, batch, *refs)
+            refs = refs[:inputs] + refs[inputs + 1 :]
+        main_kernel(windows, batch, split, *refs)
 
     return pl.pallas_call(
         body,
@@ -312,47 +325,108 @@
     )(*args)
 
 
+def taper_kernel(parts, mine, windows, row, gaps_ref, taper_ref, records_ref, *refs):
+    refs = refs if row else refs[1:]
+    outs, sems = refs[2:3] if row else refs[: len(parts)], refs[-1]
+    here = lax.axis_index("tm")
+    live, most = jnp.int32(0), gaps_ref[1, 0, 0]
+    for slot in range(1, gaps_ref.shape[2]):
+        better = gaps_ref[1, 0, slot] > most
+        live = jnp.where(better, slot, live)
+        most = jnp.where(better, gaps_ref[1, 0, slot], most)
+    start = gaps_ref[0, 0, live]
+    column = pl.ds(pl.multiple_of(live * NFFT, NFFT), NFFT)
+    copies = []
+    for n, (step, first, rows) in enumerate(parts):
+        base = pl.multiple_of(lax.rem(here + step, windows) * mine + first, SUB)
+        copies.append(pltpu.make_async_copy(records_ref.at[pl.ds(base, rows), column], outs[n], sems.at[n]))
+    if row:
+        copies.append(pltpu.make_async_copy(records_ref.at[pl.ds(0, SUB), column], refs[-2], sems.at[len(parts)]))
+    for copy in copies:
+        copy.start()
+    spots = lax.broadcasted_iota(jnp.int32, (1, NFFT), 1)
+    taper = jnp.where((spots >= start) & (spots < start + most), taper_ref[...], 0.0)
+    for n, (step, first, rows) in enumerate(parts):
+        copies[n].wait()
+        if row:
+            for v in range(RADIX):
+                column = slice(v * LANES, (v + 1) * LANES)
+                refs[0][1:, v, :] = outs[n][:, column] * taper[:, column]
+            continue
+        for r in range(0, rows, SUB):
+            outs[n][r : r + SUB, :] = outs[n][r : r + SUB, :] * taper
+    if row:
+        copies[-1].wait()
+        line = jnp.where(spots == 0, live.astype(jnp.float32), refs[-2][:1, :] * taper)
+        for v in range(RADIX):
+            refs[0][0, v : v + 1, :] = line[:, v * LANES : (v + 1) * LANES]
+            refs[1][v : v + 1, :] = line[:, v * LANES : (v + 1) * LANES]
+
+
+def tapered(records, gaps, parts, mine, windows, after=None):
+    row = after is None
+    spots = np.arange(NFFT)
+    taper = jnp.asarray((0.5 - 0.5 * np.cos(2.0 * np.pi / NFFT * spots)).astype(np.float32)[None])
+    shapes = [(rows, NFFT) for _, _, rows in parts]
+    scratch = [pltpu.SemaphoreType.DMA((len(parts) + row,))]
+    if row:
+        shapes = [(1 + SUB, RADIX, LANES), (RADIX, LANES)]
+        scratch = [pltpu.VMEM((SUB, NFFT), jnp.float32)] * 2 + scratch
+    return pl.pallas_call(
+        functools.partial(taper_kernel, parts, mine, windows, row),
+        out_shape=[jax.ShapeDtypeStruct(shape, jnp.float32) for shape in shapes],
+        in_specs=[
+            pl.BlockSpec(memory_space=pltpu.SMEM),
+            pl.BlockSpec(memory_space=pltpu.VMEM),
+            pl.BlockSpec(memory_space=pltpu.HBM),
+        ]
+        + [pl.BlockSpec(memory_space=pl.ANY)] * (not row),
+        out_specs=[pl.BlockSpec(memory_space=pltpu.VMEM) for _ in shapes],
+        scratch_shapes=scratch,
+        compiler_params=pltpu.CompilerParams(vmem_limit_bytes=16 * 2**20),
+        name="taper_row" if row else "taper",
+    )(gaps, taper, pltpu.with_memory_space_constraint(records, pltpu.HBM), *([] if row else [after]))
+
+
 def shards(records, gaps):
     width = records.shape[0]
     slots = records.shape[1] // NFFT
     windows = lax.axis_size("tm")
-    here = lax.axis_index("tm")
     mine = width // windows
-    starts, counts = gaps[0, 0], gaps[1, 0]
-    live = jnp.argmax(counts).astype(jnp.int32)
-    start, count = starts[live], counts[live]
-    spots = np.arange(NFFT)
-    taper = jnp.asarray((0.5 - 0.5 * np.cos(2.0 * np.pi / NFFT * spots)).astype(np.float32))
-    taper = jnp.where((spots >= start) & (spots < start + count), taper, 0.0)
-    frames = lax.dynamic_slice(records, (jnp.int32(0), live * NFFT), (width, NFFT))
-    tapered = jnp.where(taper == 0.0, 0.0, frames) * taper
-    parted = tapered.reshape(windows, mine, NFFT)
+    far = windows // 2
 
     def shift(array, step):
         pairs = [(i, (i + step) % windows) for i in range(windows)]
         return lax.ppermute(array, "tm", pairs)
 
-    def part(step):
-        return lax.dynamic_index_in_dim(parted, (here + step) % windows, 0, keepdims=False)
-
-    last = SUB
-    cut = mine - last
+    cut = mine - SUB
     steps = list(range(1, windows))
-    own = part(0)
-    head = [own[:cut]] + [shift(part(d)[:cut], d) for d in steps]
-    tail = [own[cut:]] + [shift(part(d)[cut:], d) for d in steps]
-
-    row = jnp.where(spots == 0, live.astype(jnp.float32), tapered[0]).reshape(RADIX, LANES)
-    rows = jnp.stack([row] + [shift(row, d) for d in steps])
+    near = [d for d in steps if d != far]
+    lead, row = tapered(records, gaps, [(far, 0, SUB)], mine, windows)
+    lead = shift(lead, far)
+    lines = [row] + [lead[0] if d == far else shift(row, d) for d in steps]
+    rows = jnp.stack(lines)
+
+    parts = [(far, SUB, cut - SUB)] + [(d, 0, mine) for d in near] + [(far, cut, SUB), (0, 0, mine)]
+    bulk = tapered(records, gaps, parts, mine, windows, row)
+    rows, lead, bulk = lax.optimization_barrier((rows, lead, bulk))
+    middle, *whole, last, own = bulk
+    middle = shift(middle, far)
+    whole = [shift(array, d) for array, d in zip(whole, near)]
+    last = shift(last, far)
     raw = lax.all_gather(rows, "blk", axis=0, tiled=False)
     raw = raw.reshape(-1, LANES)
+    head = [own] + whole[: far - 1] + [middle] + whole[far - 1 :]
+    tail = [own] + whole[: far - 1] + [last] + whole[far - 1 :]
 
     norm = 1.0 / math.sqrt(NFFT * slots * windows)
     forward, back = dft_tables()
     tables = (jnp.asarray(twist_table()), jnp.asarray(forward), jnp.asarray(back), jnp.asarray(bin_weights(norm)))
     source = source_spectra(raw, lax.axis_index("blk").astype(jnp.int32), windows, tables)
-    out = correlations(head, source, tables, mine, 0, None)
-    return correlations(tail, source, tables, mine, cut, out)
+    starts = [SUB if d == far else 0 for d in range(windows)]
+    out = correlations(head, starts, lead, source, tables, mine, 0, cut, None)
+    starts = [cut if d == far else 0 for d in range(windows)]
+    return correlations(tail, starts, None, source, tables, mine, cut, SUB, out)
 
 
 def solution(mesh):

time: 77.2 us -> 67.8 us (0.88)
  starting transfers between devices: 33.5 us -> 12.9 us
  waiting for transfers between devices: 4.4 us -> 23 us
  other arithmetic: 5.91 us -> 0.01 us
  Pallas kernels: 12.7 us -> 18.1 us
  between operations: 4.8 us -> 0.09 us
  local copies, waits for them, and re-layouts: 4.53 us -> 2.45 us
    ppermute x9 -> x7, starting transfers between devices: 33.5 us -> 12.9 us  [shift(): return lax.ppermute(array, 'tm', pairs)]
    ppermute x9 -> x7, waiting for transfers between devices: 4.4 us -> 23 us  [shift(): return lax.ppermute(array, 'tm', pairs)]
    pallas_call x0 -> x2, Pallas kernels: none -> 4.59 us  [tapered(): pl.pallas_call(functools.partial(taper_kernel, parts, mine, windows, row)...]
    slice x3 -> x1, local copies, waits for them, and re-layouts: 2.83 us -> 0.01 us  [shards(): lines = [row] + [lead[0] if d == far else shift(row, d) for d in steps]]
    mul x1 -> x0, other arithmetic: 1.8 us -> none  [shards(): tapered = jnp.where(taper == 0.0, 0.0, frames) * taper]
    unnamed x12, local copies, waits for them, and re-layouts: 1.06 us -> 2.45 us
    select_n x2 -> x0, other arithmetic: 1.38 us -> none  [the longest x1 1.35 us: shards(): taper = jnp.where((spots >= start) & (spots < start + count), taper, 0.0)]
    another operation x2 -> x1, other arithmetic: 1.38 us -> 0.01 us  [shards(): rows = jnp.stack(lines)]
  transfers between devices with their start and end apart: 9 -> 7, of which waited for: 1 -> 2; matrix products, arithmetic and copies ran while one was open for 3% -> 0% of each run, Pallas kernels for 13% -> 20%
where the time goes in v1:
time: 67.8 us; the launch traced here: 67.5 us
  waiting for transfers between devices  23 us (34%)
  Pallas kernels  18.1 us (27%)
  starting transfers between devices  12.9 us (19%)
  blocking collectives  10.9 us (16%)
  local copies, waits for them, and re-layouts  2.45 us (4%)
    ppermute x7, waiting for transfers between devices, shift(): return lax.ppermute(array, 'tm', pairs)  23 us
    ppermute x7, starting transfers between devices, shift(): return lax.ppermute(array, 'tm', pairs)  12.9 us
    all_gather x1, blocking collectives, shards(): raw = lax.all_gather(rows, 'blk', axis=0, tiled=False)  10.9 us
    pallas_call x2, Pallas kernels, correlations(): pl.pallas_call(body, out_shape=jax.ShapeDtypeStruct((total, sources, NFFT...  10.6 us
    pallas_call x2, Pallas kernels, tapered(): pl.pallas_call(functools.partial(taper_kernel, parts, mine, windows, row)...  4.59 us
    pallas_call x1, Pallas kernels, source_spectra(): pl.pallas_call(functools.partial(source_kernel, windows, group), out_shap...  2.88 us
    unnamed x12, local copies, waits for them, and re-layouts  2.45 us
  transfers between devices with their start and end apart: 7, of which 2 were waited for; matrix products, arithmetic and copies ran while one was open for 0% of the time, Pallas kernels for 20%

profile of v1, /device:TPU:0, one launch (start us, length us, event | category | flops | bytes accessed | tf_op | source)
XLA Modules:
  0.0 67.5 jit_solution(7939134040548634156)
XLA Ops:
  0.0 0.0 copy-start.4
  0.0 0.7 %copy-done.4 = f32[1,4096]{1,0:T(1,128)S(1)} copy-done((f32[1,4096]{1,0:T(1,128)S(1)}, f32[1,4096]{1,0:T(1,128)}, u32[]{:S(2)}) %copy-start.4) | copy-done | bytes 16408
  0.7 0.0 copy-start.5
  0.7 0.7 %copy-done.5 = s32[2,1,2]{2,1,0:T(1,128)S(1)} copy-done((s32[2,1,2]{2,1,0:T(1,128)S(1)}, s32[2,1,2]{2,1,0:T(1,128)}, u32[]{:S(2)}) %copy-start.5) | copy-done | bytes 40
  1.4 1.6 %taper_row.1 = (f32[9,32,128]{2,1,0:T(8,128)S(1)}, f32[32,128]{1,0:T(8,128)S(1)}) custom-call(s32[2,1,2]{2,1,0:T(1,128)S(1)} %copy-done.5, f32[1,4096]{1,0:T(1,128)S(1)} %copy-done.4, f32[128,8192]{1,0:T(8,128)} %records_ref.3), custom_call_target="tpu_custom_call" | custom-call | tf_op jit(solution)/shard_map/taper_row/pallas_call | solution.py:375
  3.0 0.0 copy-start.1
  3.0 0.0 copy-start.2
  3.0 0.0 copy-start.3
  3.0 4.1 %collective-permute-start.1 = (f32[9,32,128]{2,1,0:T(8,128)S(1)}, f32[9,32,128]{2,1,0:T(8,128)S(1)}, u32[]{:S(2)}, u32[]{:S(2)}) collective-permute-start(f32[9,32,128]{2,1,0:T(8,128)S(1)} %get-tuple-element.20), channel_id=1, source_target_pairs={{0,2},{1,3},{2,0},{3,1},{4,6},{5,7},{6,4},{7,5},{8,10},{9,11},{10,... | collective-permute-start | bytes 442376 | tf_op jit(solution)/shard_map/ppermute | solution.py:400
  7.1 1.3 %collective-permute-start.2 = (f32[32,128]{1,0:T(8,128)S(1)}, f32[32,128]{1,0:T(8,128)S(1)}, u32[]{:S(2)}, u32[]{:S(2)}) collective-permute-start(f32[32,128]{1,0:T(8,128)S(1)} %get-tuple-element.19.refs_0_), channel_id=1, source_target_pairs={{0,3},{1,0},{2,1},{3,2},{4,7},{5,4},{6,5},{7,6},{8,11},{9,8},{10,9... | collective-permute-start | bytes 49160 | tf_op jit(solution)/shard_map/ppermute | solution.py:400
  8.5 0.7 %collective-permute-start = (f32[32,128]{1,0:T(8,128)S(1)}, f32[32,128]{1,0:T(8,128)S(1)}, u32[]{:S(2)}, u32[]{:S(2)}) collective-permute-start(f32[32,128]{1,0:T(8,128)S(1)} %get-tuple-element.19.refs_0_), channel_id=1, source_target_pairs={{0,1},{1,2},{2,3},{3,0},{4,5},{5,6},{6,7},{7,4},{8,9},{9,10},{10,1... | collective-permute-start | bytes 49160 | tf_op jit(solution)/shard_map/ppermute | solution.py:400
  9.2 3.0 %taper.1 = (f32[16,4096]{1,0:T(8,128)}, f32[32,4096]{1,0:T(8,128)}, f32[32,4096]{1,0:T(8,128)S(1)}, f32[8,4096]{1,0:T(8,128)}, f32[32,4096]{1,0:T(8,128)S(1)}) custom-call(s32[2,1,2]{2,1,0:T(1,128)S(1)} %copy-done.5, f32[1,4096]{1,0:T(1,128)S(1)} %copy-done.4, f32[128,8192]{1,0:T(8,128)} %records_ref.3, f32[32,128]{1,0:T(8,128)S(1)} %get-tuple-element.19.refs_0_), custom_call_target="tpu_custom_call" | custom-call | tf_op jit(solution)/shard_map/taper/pallas_call | solution.py:375
  12.2 2.5 %collective-permute-done.1.refs_4_ = f32[9,32,128]{2,1,0:T(8,128)S(1)} collective-permute-done((f32[9,32,128]{2,1,0:T(8,128)S(1)}, f32[9,32,128]{2,1,0:T(8,128)S(1)}, u32[]{:S(2)}, u32[]{:S(2)}) %collective-permute-start.1) | collective-permute-done | bytes 147488 | tf_op jit(solution)/shard_map/ppermute | solution.py:400
  14.7 0.0 collective-permute-done.2
  14.7 0.0 collective-permute-done
  14.7 0.9 %collective-permute-start.3 = (f32[32,4096]{1,0:T(8,128)}, f32[32,4096]{1,0:T(8,128)S(1)}, u32[]{:S(2)}, u32[]{:S(2)}) collective-permute-start(f32[32,4096]{1,0:T(8,128)} %get-tuple-element.27), channel_id=1, source_target_pairs={{0,1},{1,2},{2,3},{3,0},{4,5},{5,6},{6,7},{7,4},{8,9},{9,10},{10,1... | collective-permute-start | bytes 1572872 | tf_op jit(solution)/shard_map/ppermute | solution.py:400
  15.6 3.0 %collective-permute-start.5 = (f32[32,4096]{1,0:T(8,128)S(1)}, f32[32,4096]{1,0:T(8,128)S(1)}, u32[]{:S(2)}, u32[]{:S(2)}) collective-permute-start(f32[32,4096]{1,0:T(8,128)S(1)} %get-tuple-element.29), channel_id=1, source_target_pairs={{0,3},{1,0},{2,1},{3,2},{4,7},{5,4},{6,5},{7,6},{8,11},{9,8},{10,9... | collective-permute-start | bytes 1572872 | tf_op jit(solution)/shard_map/ppermute | solution.py:400
  18.6 0.9 %collective-permute-start.6 = (f32[16,4096]{1,0:T(8,128)}, f32[16,4096]{1,0:T(8,128)S(1)}, u32[]{:S(2)}, u32[]{:S(2)}) collective-permute-start(f32[16,4096]{1,0:T(8,128)} %get-tuple-element.31), channel_id=1, source_target_pairs={{0,2},{1,3},{2,0},{3,1},{4,6},{5,7},{6,4},{7,5},{8,10},{9,11},{10,... | collective-permute-start | bytes 786440 | tf_op jit(solution)/shard_map/ppermute | solution.py:400
  19.5 2.0 %collective-permute-start.4 = (f32[8,4096]{1,0:T(8,128)}, f32[8,4096]{1,0:T(8,128)S(1)}, u32[]{:S(2)}, u32[]{:S(2)}) collective-permute-start(f32[8,4096]{1,0:T(8,128)} %get-tuple-element.28), channel_id=1, source_target_pairs={{0,2},{1,3},{2,0},{3,1},{4,6},{5,7},{6,4},{7,5},{8,10},{9,11},{10,... | collective-permute-start | bytes 393224 | tf_op jit(solution)/shard_map/ppermute | solution.py:400
  21.5 10.9 %all-gather = f32[32,32,128]{2,1,0:T(8,128)} all-gather(f32[4,32,128]{2,1,0:T(8,128)S(1)} %pad_maximum_fusion), channel_id=2, replica_groups=mesh['blk'=8,'tm'=4] {'blk'}, dimensions={0}, use_global_device_ids=true | all-gather | bytes 589824 | tf_op jit(solution)/shard_map/all_gather | solution.py:417
  32.4 2.9 %sources.1.refs_5_.refs_4_ = f32[512,256]{1,0:T(8,128)} custom-call(s32[1]{0:T(128)} %bitcast.3.me_ref, f32[1024,128]{1,0:T(8,128)} %bitcast.6, f32[34,128]{1,0:T(8,128)} %constant.17.clone.twist_ref.refs_6_.refs_5_, bf16[768,256]{1,0:T(8,128)(2,1)} %constant.18.clone.table_ref.refs_7_.refs_6_, f32[16,128]{1,0:T(8,128)} %constant.20.clone.weight_ref), custom_call_target="tpu_custom_call" | custom-call | tf_op jit(solution)/shard_map/sources/pallas_call | solution.py:269
  35.3 20.5 %collective-permute-done.6.refs_2_ = f32[16,4096]{1,0:T(8,128)S(1)} collective-permute-done((f32[16,4096]{1,0:T(8,128)}, f32[16,4096]{1,0:T(8,128)S(1)}, u32[]{:S(2)}, u32[]{:S(2)}) %collective-permute-start.6) | collective-permute-done | bytes 262176 | tf_op jit(solution)/shard_map/ppermute | solution.py:400
  55.8 0.0 collective-permute-done.3.refs_1_
  55.8 0.0 collective-permute-done.5.refs_3_
  55.8 0.0 copy-done.1
  55.8 0.0 copy-done.2
  55.8 0.0 copy-done.3
  55.8 0.0 copy-start
  55.8 1.0 %copy-done = f32[512,256]{1,0:T(8,128)S(1)} copy-done((f32[512,256]{1,0:T(8,128)S(1)}, f32[512,256]{1,0:T(8,128)}, u32[]{:S(2)}) %copy-start) | copy-done | bytes 524312
  56.9 7.5 %lags_0.1.refs_8_ = f32[32,8,4096]{2,1,0:T(8,128)} custom-call(f32[32,4096]{1,0:T(8,128)S(1)} %get-tuple-element.26.refs_0_, f32[32,4096]{1,0:T(8,128)S(1)} %collective-permute-done.3.refs_1_, f32[16,4096]{1,0:T(8,128)S(1)} %collective-permute-done.6.refs_2_, f32[32,4096]{1,0:T(8,128)S(1)} %collective-permute-done.5.refs_3_, ...), custom_call_target="tpu_custom_call" | custom-call | tf_op jit(solution)/shard_map/lags_0/pallas_call | solution.py:311
  64.4 0.0 collective-permute-done.4.refs_2_
  64.4 3.1 %lags_24.1 = f32[32,8,4096]{2,1,0:T(8,128)} custom-call(f32[32,4096]{1,0:T(8,128)S(1)} %get-tuple-element.26.refs_0_, f32[32,4096]{1,0:T(8,128)S(1)} %collective-permute-done.3.refs_1_, f32[8,4096]{1,0:T(8,128)S(1)} %collective-permute-done.4.refs_2_, f32[32,4096]{1,0:T(8,128)S(1)} %collective-permute-done.5.refs_3_, ...), custom_call_target="tpu_custom_call", output_to_operand_aliasing={{}: (8, {})} | custom-call | tf_op jit(solution)/shard_map/lags_24/pallas_call | solution.py:311
  (2 shorter events, 0.0 us)
Async XLA Ops:
  0.0 0.7 %copy-start.4 = (f32[1,4096]{1,0:T(1,128)S(1)}, f32[1,4096]{1,0:T(1,128)}, u32[]{:S(2)}) copy-start(f32[1,4096]{1,0:T(1,128)} %constant.16.clone.taper_ref) | copy-start | bytes 49156
  0.7 0.7 %copy-start.5 = (s32[2,1,2]{2,1,0:T(1,128)S(1)}, s32[2,1,2]{2,1,0:T(1,128)}, u32[]{:S(2)}) copy-start(s32[2,1,2]{2,1,0:T(1,128)} %gaps_ref.3) | copy-start | bytes 52
  3.0 52.8 %copy-start.1 = (bf16[768,256]{1,0:T(8,128)(2,1)S(1)}, bf16[768,256]{1,0:T(8,128)(2,1)}, u32[]{:S(2)}) copy-start(bf16[768,256]{1,0:T(8,128)(2,1)} %constant.18.clone.table_ref.refs_7_.refs_6_) | copy-start | bytes 1179652
  3.0 52.8 %copy-start.2 = (bf16[768,256]{1,0:T(8,128)(2,1)S(1)}, bf16[768,256]{1,0:T(8,128)(2,1)}, u32[]{:S(2)}) copy-start(bf16[768,256]{1,0:T(8,128)(2,1)} %constant.19.clone.refs_8_.refs_7_) | copy-start | bytes 1179652
  3.0 52.8 %copy-start.3 = (f32[34,128]{1,0:T(8,128)S(1)}, f32[34,128]{1,0:T(8,128)}, u32[]{:S(2)}) copy-start(f32[34,128]{1,0:T(8,128)} %constant.17.clone.twist_ref.refs_6_.refs_5_) | copy-start | bytes 52228
  3.0 11.6 %collective-permute-start.1 = (f32[9,32,128]{2,1,0:T(8,128)S(1)}, f32[9,32,128]{2,1,0:T(8,128)S(1)}, u32[]{:S(2)}, u32[]{:S(2)}) collective-permute-start(f32[9,32,128]{2,1,0:T(8,128)S(1)} %get-tuple-element.20), channel_id=1, source_target_pairs={{0,2},{1,3},{2,0},{3,1},{4,6},{5,7},{6,4},{7,5},{8,10},{9,11},{10,... | collective-permute-start | bytes 442376 | tf_op jit(solution)/shard_map/ppermute | solution.py:400
  7.1 7.5 %collective-permute-start.2 = (f32[32,128]{1,0:T(8,128)S(1)}, f32[32,128]{1,0:T(8,128)S(1)}, u32[]{:S(2)}, u32[]{:S(2)}) collective-permute-start(f32[32,128]{1,0:T(8,128)S(1)} %get-tuple-element.19.refs_0_), channel_id=1, source_target_pairs={{0,3},{1,0},{2,1},{3,2},{4,7},{5,4},{6,5},{7,6},{8,11},{9,8},{10,9... | collective-permute-start | bytes 49160 | tf_op jit(solution)/shard_map/ppermute | solution.py:400
  8.5 6.2 %collective-permute-start = (f32[32,128]{1,0:T(8,128)S(1)}, f32[32,128]{1,0:T(8,128)S(1)}, u32[]{:S(2)}, u32[]{:S(2)}) collective-permute-start(f32[32,128]{1,0:T(8,128)S(1)} %get-tuple-element.19.refs_0_), channel_id=1, source_target_pairs={{0,1},{1,2},{2,3},{3,0},{4,5},{5,6},{6,7},{7,4},{8,9},{9,10},{10,1... | collective-permute-start | bytes 49160 | tf_op jit(solution)/shard_map/ppermute | solution.py:400
  14.7 41.1 %collective-permute-start.3 = (f32[32,4096]{1,0:T(8,128)}, f32[32,4096]{1,0:T(8,128)S(1)}, u32[]{:S(2)}, u32[]{:S(2)}) collective-permute-start(f32[32,4096]{1,0:T(8,128)} %get-tuple-element.27), channel_id=1, source_target_pairs={{0,1},{1,2},{2,3},{3,0},{4,5},{5,6},{6,7},{7,4},{8,9},{9,10},{10,1... | collective-permute-start | bytes 1572872 | tf_op jit(solution)/shard_map/ppermute | solution.py:400
  15.6 40.2 %collective-permute-start.5 = (f32[32,4096]{1,0:T(8,128)S(1)}, f32[32,4096]{1,0:T(8,128)S(1)}, u32[]{:S(2)}, u32[]{:S(2)}) collective-permute-start(f32[32,4096]{1,0:T(8,128)S(1)} %get-tuple-element.29), channel_id=1, source_target_pairs={{0,3},{1,0},{2,1},{3,2},{4,7},{5,4},{6,5},{7,6},{8,11},{9,8},{10,9... | collective-permute-start | bytes 1572872 | tf_op jit(solution)/shard_map/ppermute | solution.py:400
  18.6 37.2 %collective-permute-start.6 = (f32[16,4096]{1,0:T(8,128)}, f32[16,4096]{1,0:T(8,128)S(1)}, u32[]{:S(2)}, u32[]{:S(2)}) collective-permute-start(f32[16,4096]{1,0:T(8,128)} %get-tuple-element.31), channel_id=1, source_target_pairs={{0,2},{1,3},{2,0},{3,1},{4,6},{5,7},{6,4},{7,5},{8,10},{9,11},{10,... | collective-permute-start | bytes 786440 | tf_op jit(solution)/shard_map/ppermute | solution.py:400
  19.5 44.9 %collective-permute-start.4 = (f32[8,4096]{1,0:T(8,128)}, f32[8,4096]{1,0:T(8,128)S(1)}, u32[]{:S(2)}, u32[]{:S(2)}) collective-permute-start(f32[8,4096]{1,0:T(8,128)} %get-tuple-element.28), channel_id=1, source_target_pairs={{0,2},{1,3},{2,0},{3,1},{4,6},{5,7},{6,4},{7,5},{8,10},{9,11},{10,... | collective-permute-start | bytes 393224 | tf_op jit(solution)/shard_map/ppermute | solution.py:400
  55.8 1.0 %copy-start = (f32[512,256]{1,0:T(8,128)S(1)}, f32[512,256]{1,0:T(8,128)}, u32[]{:S(2)}) copy-start(f32[512,256]{1,0:T(8,128)} %sources.1.refs_5_.refs_4_) | copy-start | bytes 1572868

commit v2 on v0

--- a/solution.py
+++ b/solution.py
@@ -160,37 +160,54 @@
     return [r * scale for r in re], [i * scale for i in im]
 
 
-def source_kernel(windows, group, me_ref, raw_ref, twist_ref, table_ref, weight_ref, out_ref, grid_ref):
-    sources = raw_ref.shape[0] // (windows * RADIX)
+def source_stage(windows, me, raw_ref, twist_ref, table_ref, weight_ref, out_ref, grid_ref):
+    span = windows * RADIX
+    sources = raw_ref.shape[0] // span
     lanes = lane_ids()
-    me = me_ref[0]
-    span = windows * RADIX
-    for w in range(windows):
-        own = jnp.broadcast_to(raw_ref[pl.ds(me * span + w * RADIX, 1), :1], (SUB, 1))
-        for g in range(sources // group):
-            x = [raw_ref[pl.ds(g * group * span + w * RADIX + v, SUB, stride=span), :] for v in range(RADIX)]
-            match = jnp.where(x[0][:, :1] == own, 1.0, 0.0)
+    for g in range(sources // SUB):
+        match = []
+        for w in range(windows):
+            own = jnp.broadcast_to(raw_ref[pl.ds(me * span + w * RADIX, 1), :1], (SUB, 1))
+            x = [raw_ref[pl.ds(g * SUB * span + w * RADIX + v, SUB, stride=span), :] for v in range(RADIX)]
+            match.append(jnp.where(x[0][:, :1] == own, 1.0, 0.0))
             x[0] = jnp.where(lanes == 0, 0.0, x[0])
-            lift(x, twist_ref, grid_ref, 0)
-            grid_ref[...] = matmul(grid_ref[...], table_ref[...])
-            re, im = whiten(grid_ref, 0)
+            lift(x, twist_ref, grid_ref, w * PAD)
+        grid_ref[...] = matmul(grid_ref[...], table_ref[...])
+        for w in range(windows):
+            re, im = whiten(grid_ref, w * PAD)
             for k in range(HALF):
-                weight = weight_ref[k : k + 1, :] * match
-                spot = pl.ds((w * HALF + k) * sources + g * group, SUB)
+                weight = weight_ref[k : k + 1, :] * match[w]
+                spot = pl.ds((w * HALF + k) * sources + g * SUB, SUB)
                 out_ref[spot, :LANES] = re[k] * weight
                 out_ref[spot, LANES:] = im[k] * weight
 
 
-def main_kernel(windows, batch, *refs):
-    ins, (source_ref, twist_ref, table_ref, back_ref, out_ref, grid_ref, spec_ref, cross_ref) = refs[:windows], refs[windows:]
-    group = pl.program_id(1)
+def main_kernel(windows, batch, first, blocks, bases, *refs):
+    fresh = len(refs) - windows - 4 == 11
+    ins, refs = refs[:windows], refs[windows:]
+    twist_ref, table_ref, back_ref, weight_ref = refs[:4]
+    if fresh:
+        raw_hbm, out_ref, kept_ref, source_ref, grid_ref, spec_ref, cross_ref, page_ref, raw_ref, sems, load = refs[4:]
+    else:
+        kept_ref, _, out_ref, source_ref, grid_ref, spec_ref, cross_ref, page_ref, sems, load = refs[4:]
     sources = source_ref.shape[0] // (windows * HALF)
-    first = lane_ids() < QUART
-
-    @pl.when(group == 0)
-    def _():
+    if fresh:
+        fetch = pltpu.make_async_copy(raw_hbm, raw_ref, load.at[0])
+        keep = pltpu.make_async_copy(source_ref, kept_ref, load.at[1])
+    else:
+        fetch = pltpu.make_async_copy(kept_ref, source_ref, load.at[0])
+    fetch.start()
+    lower = lane_ids() < QUART
+    rounds = SUB // batch
+    steps = rounds * (sources // SUB)
+
+    def forward(block):
         for w in range(windows):
-            x = [ins[w][:, v * LANES : (v + 1) * LANES] for v in range(RADIX)]
+            if bases[w] is None:
+                x = [ins[w][RADIX + v * SUB : RADIX + (v + 1) * SUB, :] for v in range(RADIX)]
+            else:
+                spot = pl.ds(pl.multiple_of(bases[w] + block * SUB, SUB), SUB)
+                x = [ins[w][spot, v * LANES : (v + 1) * LANES] for v in range(RADIX)]
             lift(x, twist_ref, grid_ref, w * PAD)
         grid_ref[...] = matmul(grid_ref[...], table_ref[...])
         for w in range(windows):
@@ -199,14 +216,36 @@
                 spec_ref[:, w * HALF + k, :LANES] = re[k]
                 spec_ref[:, w * HALF + k, LANES:] = im[k]
 
+    def place(step):
+        block, within = lax.div(step, steps), lax.rem(step, steps)
+        return block, lax.rem(within, rounds) * batch, pl.multiple_of(lax.div(within, rounds) * SUB, SUB)
+
+    def copy(step, slot, c):
+        block, start, group = place(step)
+        target = out_ref.at[first + block * SUB + start + c, pl.ds(group, SUB), :]
+        return pltpu.make_async_copy(page_ref.at[slot, c], target, sems.at[slot, c])
+
     def some(step, _):
-        start = step * batch
+        slot = lax.rem(step, 2)
+        block, start, group = place(step)
+
+        @pl.when(lax.rem(step, steps) == 0)
+        def _():
+            forward(block)
+
+        if not fresh:
+            pl.when(step == 0)(fetch.wait)
+
+        @pl.when(step >= 2)
+        def _():
+            for c in range(batch):
+                copy(step - 2, slot, c).wait()
 
         def combine(k):
             found = []
             parts = []
             for w in range(windows):
-                spot = pl.ds((w * HALF + k) * sources + group * SUB, SUB)
+                spot = pl.ds(pl.multiple_of((w * HALF + k) * sources + group, SUB), SUB)
                 parts.append((source_ref[spot, :LANES], source_ref[spot, LANES:]))
             for c in range(batch):
                 re = im = None
@@ -221,10 +260,10 @@
             return found
 
         for c, (re, im) in enumerate(combine(0)):
-            cross_ref[pl.ds(c * PAD, SUB), :LANES] = jnp.where(first, re, 0.0)
-            cross_ref[pl.ds(c * PAD, SUB), LANES:] = jnp.where(first, im, 0.0)
-            cross_ref[pl.ds(c * PAD + HALF * SUB, SUB), :LANES] = jnp.where(first, 0.0, re)
-            cross_ref[pl.ds(c * PAD + HALF * SUB, SUB), LANES:] = jnp.where(first, 0.0, im)
+            cross_ref[pl.ds(c * PAD, SUB), :LANES] = jnp.where(lower, re, 0.0)
+            cross_ref[pl.ds(c * PAD, SUB), LANES:] = jnp.where(lower, im, 0.0)
+            cross_ref[pl.ds(c * PAD + HALF * SUB, SUB), :LANES] = jnp.where(lower, 0.0, re)
+            cross_ref[pl.ds(c * PAD + HALF * SUB, SUB), LANES:] = jnp.where(lower, 0.0, im)
         for k in range(1, HALF):
             for c, (re, im) in enumerate(combine(k)):
                 spot = pl.ds(c * PAD + k * SUB, SUB)
@@ -246,69 +285,139 @@
                 im.append(i)
             lags = real_fft_adjoint(re, im)
             for v in range(RADIX):
-                out_ref[start + c, :, v * LANES : (v + 1) * LANES] = lags[v]
+                page_ref[slot, c, :, v * LANES : (v + 1) * LANES] = lags[v]
+            copy(step, slot, c).start()
         return 0
 
-    lax.fori_loop(0, SUB // batch, some, 0)
-
-
-def resident(array):
-    return pl.BlockSpec(array.shape, lambda *_: (0,) * array.ndim)
-
-
-def source_spectra(raw, me, windows, tables):
-    twist, forward, _, weights = tables
-    sources = raw.shape[0] // (windows * RADIX)
-    group = SUB
-    shape = (windows * HALF * sources, 2 * LANES)
+    if fresh:
+        fetch.wait()
+        source_stage(windows, lax.axis_index("blk"), raw_ref, twist_ref, table_ref, weight_ref, source_ref, grid_ref)
+        keep.start()
+    every = steps * blocks
+    lax.fori_loop(0, every, some, 0)
+    for step in range(max(0, every - 2), every):
+        for c in range(batch):
+            copy(jnp.int32(step), step % 2, c).wait()
+    if fresh:
+        keep.wait()
+
+
+def correlations(pieces, tables, total, first, rows, raw=None, source=None, before=None, batch=4):
+    windows = len(pieces)
+    sources = raw.shape[0] // (windows * RADIX) if source is None else source.shape[0] // (windows * HALF)
+    args = [array for array, _ in pieces] + list(tables)
+    inside, outside = pl.BlockSpec(memory_space=pltpu.VMEM), pl.BlockSpec(memory_space=pltpu.HBM)
+    specs = [inside] * len(args)
+    shapes = [jax.ShapeDtypeStruct((total, sources, NFFT), jnp.float32)]
+    spectra = (windows * HALF * sources, 2 * LANES)
+    scratch = [
+        pltpu.VMEM(spectra, jnp.float32),
+        pltpu.VMEM((windows * PAD, 2 * LANES), jnp.float32),
+        pltpu.VMEM((SUB, windows * HALF, 2 * LANES), jnp.float32),
+        pltpu.VMEM((batch * PAD, 2 * LANES), jnp.float32),
+        pltpu.VMEM((2, batch, SUB, NFFT), jnp.float32),
+        pltpu.SemaphoreType.DMA((2, batch)),
+        pltpu.SemaphoreType.DMA((2,)),
+    ]
+    aliases = {}
+    if source is None:
+        args.append(raw)
+        specs.append(outside)
+        shapes.append(jax.ShapeDtypeStruct(spectra, jnp.float32))
+        scratch.insert(5, pltpu.VMEM(raw.shape, jnp.float32))
+    else:
+        aliases = {len(args) + 1: 0}
+        args += [source, before]
+        specs += [outside, pl.BlockSpec(memory_space=pl.ANY)]
     return pl.pallas_call(
-        functools.partial(source_kernel, windows, group),
-        out_shape=jax.ShapeDtypeStruct(shape, jnp.float32),
-        grid_spec=pltpu.PrefetchScalarGridSpec(
-            num_scalar_prefetch=1,
-            grid=(1,),
-            in_specs=[resident(raw), resident(twist), resident(forward), resident(weights)],
-            out_specs=pl.BlockSpec(shape, lambda *_: (0, 0)),
-            scratch_shapes=[pltpu.VMEM((PAD, 2 * LANES), jnp.float32)],
-        ),
-        name="sources",
-    )(me.reshape(1), raw, twist, forward, weights)
-
-
-def correlations(pieces, source, tables, total, first, before, batch=4):
-    twist, forward, back, _ = tables
-    windows = len(pieces)
-    sources = source.shape[0] // (windows * HALF)
-    rows = pieces[0].shape[0]
-    offset = first // SUB
-    args = [*pieces, source, twist, forward, back]
-    specs = [pl.BlockSpec((SUB, NFFT), lambda c, g: (c, 0))] * windows
-    specs += [resident(a) for a in args[windows:]]
-    aliases = {}
-    if before is not None:
-        aliases = {len(args): 0}
-        args.append(before)
-        specs.append(pl.BlockSpec(memory_space=pl.ANY))
-
-    def body(*refs):
-        if before is not None:
-            refs = refs[: windows + 4] + refs[windows + 5 :]
-        main_kernel(windows, batch, *refs)
-
+        functools.partial(main_kernel, windows, batch, first, rows // SUB, [base for _, base in pieces]),
+        out_shape=shapes,
+        in_specs=specs,
+        out_specs=[outside] * len(shapes),
+        scratch_shapes=scratch,
+        input_output_aliases=aliases,
+        compiler_params=pltpu.CompilerParams(vmem_limit_bytes=32 * 2**20),
+        name=f"lags_{first}",
+    )(*args)
+
+
+def all_tables(norm):
+    forward, back = dft_tables()
+    return tuple(jnp.asarray(table) for table in (twist_table(), forward, back, bin_weights(norm)))
+
+
+def live_window(gaps_ref):
+    live, most = jnp.int32(0), gaps_ref[1, 0, 0]
+    for slot in range(1, gaps_ref.shape[2]):
+        better = gaps_ref[1, 0, slot] > most
+        live = jnp.where(better, slot, live)
+        most = jnp.where(better, gaps_ref[1, 0, slot], most)
+    return live, gaps_ref[0, 0, live], most
+
+
+def taper_kernel(mine, windows, lead, rest, gaps_hbm, taper_hbm, records_ref, *refs):
+    outs, (gaps_ref, taper_ref, head_ref, load, sems) = refs[:-5], refs[-5:]
+    here = lax.axis_index("tm")
+    known = pltpu.make_async_copy(gaps_hbm, gaps_ref, load.at[0])
+    shape = pltpu.make_async_copy(taper_hbm, taper_ref, load.at[1])
+    known.start()
+    shape.start()
+    heads = [lax.rem(here + step, windows) * mine for step in lead] + [jnp.int32(0)] * bool(lead)
+    copies = []
+    for slot in range(gaps_ref.shape[2] if lead else 0):
+        for n, base in enumerate(heads):
+            spot = pl.ds(pl.multiple_of(base, SUB), SUB)
+            source = records_ref.at[spot, pl.ds(slot * NFFT, NFFT)]
+            copies.append(pltpu.make_async_copy(source, head_ref.at[slot, n], sems.at[len(copies)]))
+    for copy in copies:
+        copy.start()
+    known.wait()
+    live, start, most = live_window(gaps_ref)
+    column = pl.ds(pl.multiple_of(live * NFFT, NFFT), NFFT)
+    for n, (step, first, rows) in enumerate(rest):
+        base = pl.multiple_of(lax.rem(here + step, windows) * mine + first, SUB)
+        copies.append(pltpu.make_async_copy(records_ref.at[pl.ds(base, rows), column], outs[n], sems.at[n]))
+        copies[-1].start()
+    shape.wait()
+    spots = lax.broadcasted_iota(jnp.int32, (1, NFFT), 1)
+    taper = jnp.where((spots >= start) & (spots < start + most), taper_ref[...], 0.0)
+    if lead:
+        for copy in copies:
+            copy.wait()
+        line = jnp.where(spots == 0, live.astype(jnp.float32), head_ref[live, len(lead), :1, :] * taper)
+        for v in range(RADIX):
+            lanes = slice(v * LANES, (v + 1) * LANES)
+            for n in range(len(lead)):
+                outs[n][v : v + 1, :] = line[:, lanes]
+                outs[n][RADIX + v * SUB : RADIX + (v + 1) * SUB, :] = head_ref[live, n, :, lanes] * taper[:, lanes]
+            outs[len(lead)][v : v + 1, :] = line[:, lanes]
+        return
+    for n, copy in enumerate(copies):
+        copy.wait()
+        for r in range(0, outs[n].shape[0], SUB):
+            outs[n][r : r + SUB, :] = outs[n][r : r + SUB, :] * taper
+
+
+def tapered(records, gaps, mine, windows, lead, rest):
+    spots = np.arange(NFFT)
+    slots = gaps.shape[2]
+    taper = jnp.asarray((0.5 - 0.5 * np.cos(2.0 * np.pi / NFFT * spots)).astype(np.float32)[None])
+    shapes = [(RADIX * (1 + SUB), LANES)] * len(lead) + [(RADIX, LANES)] * bool(lead) + [(rows, NFFT) for _, _, rows in rest]
+    args = [pltpu.with_memory_space_constraint(array, pltpu.HBM) for array in (gaps, taper, records)]
     return pl.pallas_call(
-        body,
-        out_shape=jax.ShapeDtypeStruct((total, sources, NFFT), jnp.float32),
-        grid=(rows // SUB, sources // SUB),
-        in_specs=specs,
-        out_specs=pl.BlockSpec((SUB, SUB, NFFT), lambda c, g: (c + offset, g, 0)),
+        functools.partial(taper_kernel, mine, windows, lead, rest),
+        out_shape=[jax.ShapeDtypeStruct(shape, jnp.float32) for shape in shapes],
+        in_specs=[pl.BlockSpec(memory_space=pltpu.HBM)] * 3,
+        out_specs=[pl.BlockSpec(memory_space=pltpu.VMEM) for _ in shapes],
         scratch_shapes=[
-            pltpu.VMEM((windows * PAD, 2 * LANES), jnp.float32),
-            pltpu.VMEM((SUB, windows * HALF, 2 * LANES), jnp.float32),
-            pltpu.VMEM((batch * PAD, 2 * LANES), jnp.float32),
+            pltpu.SMEM(gaps.shape, jnp.int32),
+            pltpu.VMEM(taper.shape, jnp.float32),
+            pltpu.VMEM((slots, 1 + len(lead), SUB, NFFT), jnp.float32),
+            pltpu.SemaphoreType.DMA((2,)),
+            pltpu.SemaphoreType.DMA((max(len(rest), slots * (1 + len(lead))),)),
         ],
-        input_output_aliases=aliases,
-        compiler_params=pltpu.CompilerParams(vmem_limit_bytes=40 * 2**20),
-        name=f"lags_{first}",
+        compiler_params=pltpu.CompilerParams(vmem_limit_bytes=16 * 2**20),
+        name="taper_lead" if lead else "taper",
     )(*args)
 
 
@@ -316,43 +425,37 @@
     width = records.shape[0]
     slots = records.shape[1] // NFFT
     windows = lax.axis_size("tm")
-    here = lax.axis_index("tm")
     mine = width // windows
-    starts, counts = gaps[0, 0], gaps[1, 0]
-    live = jnp.argmax(counts).astype(jnp.int32)
-    start, count = starts[live], counts[live]
-    spots = np.arange(NFFT)
-    taper = jnp.asarray((0.5 - 0.5 * np.cos(2.0 * np.pi / NFFT * spots)).astype(np.float32))
-    taper = jnp.where((spots >= start) & (spots < start + count), taper, 0.0)
-    frames = lax.dynamic_slice(records, (jnp.int32(0), live * NFFT), (width, NFFT))
-    tapered = jnp.where(taper == 0.0, 0.0, frames) * taper
-    parted = tapered.reshape(windows, mine, NFFT)
+    cut = mine - SUB
 
     def shift(array, step):
         pairs = [(i, (i + step) % windows) for i in range(windows)]
         return lax.ppermute(array, "tm", pairs)
 
-    def part(step):
-        return lax.dynamic_index_in_dim(parted, (here + step) % windows, 0, keepdims=False)
-
-    last = SUB
-    cut = mine - last
     steps = list(range(1, windows))
-    own = part(0)
-    head = [own[:cut]] + [shift(part(d)[:cut], d) for d in steps]
-    tail = [own[cut:]] + [shift(part(d)[cut:], d) for d in steps]
-
-    row = jnp.where(spots == 0, live.astype(jnp.float32), tapered[0]).reshape(RADIX, LANES)
-    rows = jnp.stack([row] + [shift(row, d) for d in steps])
+    order = sorted(steps, key=lambda d: -min(d, windows - d))
+    *lead, row = tapered(records, gaps, mine, windows, steps, [])
+    lead = dict(zip(steps, lead))
+    lead = {d: shift(lead[d], d) for d in order}
+    rows = jnp.stack([row] + [lead[d][:RADIX] for d in steps])
+
+    single, split = order[-1], order[:-1]
+    rest = [(d, SUB, cut - SUB) for d in split] + [(single, SUB, mine - SUB)] + [(d, cut, SUB) for d in split] + [(0, 0, mine)]
+    *bulk, own = tapered(records, gaps, mine, windows, [], rest)
+    early, late = bulk[: len(steps)], bulk[len(steps) :]
+    rows, late = lax.optimization_barrier((rows, late))
     raw = lax.all_gather(rows, "blk", axis=0, tiled=False)
     raw = raw.reshape(-1, LANES)
-
-    norm = 1.0 / math.sqrt(NFFT * slots * windows)
-    forward, back = dft_tables()
-    tables = (jnp.asarray(twist_table()), jnp.asarray(forward), jnp.asarray(back), jnp.asarray(bin_weights(norm)))
-    source = source_spectra(raw, lax.axis_index("blk").astype(jnp.int32), windows, tables)
-    out = correlations(head, source, tables, mine, 0, None)
-    return correlations(tail, source, tables, mine, cut, out)
+    early = {d: shift(array, d) for d, array in zip(order, early)}
+    late = {d: shift(array, d) for d, array in zip(split, late)}
+
+    tables = all_tables(1.0 / math.sqrt(NFFT * slots * windows))
+    pieces = [(own, 0)] + [(lead[d], None) for d in steps]
+    more = [(own, SUB)] + [(early[d], 0) for d in steps]
+    out, source = correlations(pieces, tables, mine, 0, SUB, raw=raw)
+    (out,) = correlations(more, tables, mine, SUB, cut - SUB, source=source, before=out)
+    pieces = [(own, cut)] + [(late[d], 0) if d in late else (early[d], cut - SUB) for d in steps]
+    return correlations(pieces, tables, mine, cut, SUB, source=source, before=out)[0]
 
 
 def solution(mesh):

time: 77.2 us -> 56.8 us (0.74)
  starting transfers between devices: 33.5 us -> 15.4 us
  waiting for transfers between devices: 4.4 us -> 15.8 us
  other arithmetic: 5.91 us -> 0.01 us
  between operations: 4.8 us -> 0.09 us
  local copies, waits for them, and re-layouts: 4.53 us -> 0.02 us
  Pallas kernels: 12.7 us -> 15.5 us
  blocking collectives: 10.9 us -> 9.85 us
    ppermute x9 -> x8, starting transfers between devices: 33.5 us -> 15.4 us  [shift(): return lax.ppermute(array, 'tm', pairs)]
    ppermute x9 -> x8, waiting for transfers between devices: 4.4 us -> 15.8 us  [shift(): return lax.ppermute(array, 'tm', pairs)]
    slice x3 -> x0, local copies, waits for them, and re-layouts: 2.83 us -> none  [the longest x1 1.13 us: shards(): tail = [own[cut:]] + [shift(part(d)[cut:], d) for d in steps]]
    pallas_call x3 -> x5, Pallas kernels: 12.7 us -> 15.5 us  [the longest x3 11.8 us: correlations(): pl.pallas_call(functools.partial(main_kernel, windows, batch, first, rows...]
    mul x1 -> x0, other arithmetic: 1.8 us -> none  [shards(): tapered = jnp.where(taper == 0.0, 0.0, frames) * taper]
    select_n x2 -> x0, other arithmetic: 1.38 us -> none  [the longest x1 1.35 us: shards(): taper = jnp.where((spots >= start) & (spots < start + count), taper, 0.0)]
    another operation x2 -> x1, other arithmetic: 1.38 us -> 0.01 us  [shards(): rows = jnp.stack([row] + [lead[d][:RADIX] for d in steps])]
    eq x1 -> x0, other arithmetic: 1.35 us -> none  [shards(): tapered = jnp.where(taper == 0.0, 0.0, frames) * taper]
  transfers between devices with their start and end apart: 9 -> 8, of which waited for: 1 -> 2; matrix products, arithmetic and copies ran while one was open for 3% -> 0% of each run, Pallas kernels for 13% -> 20%
where the time goes in v2:
time: 56.8 us; the launch traced here: 56.6 us
  waiting for transfers between devices  15.8 us (28%)
  Pallas kernels  15.5 us (27%)
  starting transfers between devices  15.4 us (27%)
  blocking collectives  9.85 us (17%)
    ppermute x8, waiting for transfers between devices, shift(): return lax.ppermute(array, 'tm', pairs)  15.8 us
    ppermute x8, starting transfers between devices, shift(): return lax.ppermute(array, 'tm', pairs)  15.4 us
    pallas_call x3, Pallas kernels, correlations(): pl.pallas_call(functools.partial(main_kernel, windows, batch, first, rows...  11.8 us
    all_gather x1, blocking collectives, shards(): raw = lax.all_gather(rows, 'blk', axis=0, tiled=False)  9.85 us
    pallas_call x2, Pallas kernels, tapered(): pl.pallas_call(functools.partial(taper_kernel, mine, windows, lead, rest)...  3.71 us
  transfers between devices with their start and end apart: 8, of which 2 were waited for; matrix products, arithmetic and copies ran while one was open for 0% of the time, Pallas kernels for 20%

profile of v2, /device:TPU:0, one launch (start us, length us, event | category | flops | bytes accessed | tf_op | source)
XLA Modules:
  0.0 56.6 jit_solution(12809796981283516002)
XLA Ops:
  0.0 0.0 copy-start
  0.0 0.0 copy-start.1
  0.0 0.0 copy-start.2
  0.0 0.0 copy-start.3
  0.0 1.5 %taper_lead.1 = (f32[288,128]{1,0:T(8,128)S(1)}, f32[288,128]{1,0:T(8,128)S(1)}, f32[288,128]{1,0:T(8,128)S(1)}, f32[32,128]{1,0:T(8,128)S(1)}) custom-call(s32[2,1,2]{2,1,0:T(1,128)} %gaps_hbm.3, f32[1,4096]{1,0:T(1,128)} %constant.10.clone.taper_hbm, f32[128,8192]{1,0:T(8,128)} %records_ref.3), custom_call_target="tpu_custom_call" | custom-call | tf_op jit(solution)/shard_map/taper_lead/pallas_call | solution.py:407
  1.5 3.1 %collective-permute-start = (f32[288,128]{1,0:T(8,128)S(1)}, f32[288,128]{1,0:T(8,128)S(1)}, u32[]{:S(2)}, u32[]{:S(2)}) collective-permute-start(f32[288,128]{1,0:T(8,128)S(1)} %get-tuple-element.22), channel_id=1, source_target_pairs={{0,1},{1,2},{2,3},{3,0},{4,5},{5,6},{6,7},{7,4},{8,9},{9,10},{10,1... | collective-permute-start | bytes 442376 | tf_op jit(solution)/shard_map/ppermute | solution.py:433
  4.6 2.6 %collective-permute-start.1 = (f32[288,128]{1,0:T(8,128)S(1)}, f32[288,128]{1,0:T(8,128)S(1)}, u32[]{:S(2)}, u32[]{:S(2)}) collective-permute-start(f32[288,128]{1,0:T(8,128)S(1)} %get-tuple-element.23), channel_id=1, source_target_pairs={{0,2},{1,3},{2,0},{3,1},{4,6},{5,7},{6,4},{7,5},{8,10},{9,11},{10,... | collective-permute-start | bytes 442376 | tf_op jit(solution)/shard_map/ppermute | solution.py:433
  7.2 1.3 %collective-permute-start.2 = (f32[288,128]{1,0:T(8,128)S(1)}, f32[288,128]{1,0:T(8,128)S(1)}, u32[]{:S(2)}, u32[]{:S(2)}) collective-permute-start(f32[288,128]{1,0:T(8,128)S(1)} %get-tuple-element.24), channel_id=1, source_target_pairs={{0,3},{1,0},{2,1},{3,2},{4,7},{5,4},{6,5},{7,6},{8,11},{9,8},{10,9... | collective-permute-start | bytes 442376 | tf_op jit(solution)/shard_map/ppermute | solution.py:433
  8.6 2.2 %taper.1 = (f32[16,4096]{1,0:T(8,128)S(1)}, f32[16,4096]{1,0:T(8,128)S(1)}, f32[24,4096]{1,0:T(8,128)S(1)}, f32[8,4096]{1,0:T(8,128)S(1)}, f32[8,4096]{1,0:T(8,128)S(1)}, /*index=5*/f32[32,4096]{1,0:T(8,128)S(1)}) custom-call(s32[2,1,2]{2,1,0:T(1,128)} %gaps_hbm.3, f32[1,4096]{1,0:T(1,128)} %constant.10.clone.taper_hbm, f32[128,8192]{1,0:T(8,128)} %records_ref.3), custom_call_target="tpu_custom_call" | custom-call | tf_op jit(solution)/shard_map/taper/pallas_call | solution.py:407
  10.8 0.7 %collective-permute-start.6 = (f32[16,4096]{1,0:T(8,128)S(1)}, f32[16,4096]{1,0:T(8,128)S(1)}, u32[]{:S(2)}, u32[]{:S(2)}) collective-permute-start(f32[16,4096]{1,0:T(8,128)S(1)} %get-tuple-element.32), channel_id=1, source_target_pairs={{0,1},{1,2},{2,3},{3,0},{4,5},{5,6},{6,7},{7,4},{8,9},{9,10},{10,1... | collective-permute-start | bytes 786440 | tf_op jit(solution)/shard_map/ppermute | solution.py:433
  11.5 0.3 collective-permute-start.7
  11.8 0.0 collective-permute-done.refs_1_
  11.8 2.8 %collective-permute-start.5 = (f32[24,4096]{1,0:T(8,128)S(1)}, f32[24,4096]{1,0:T(8,128)S(1)}, u32[]{:S(2)}, u32[]{:S(2)}) collective-permute-start(f32[24,4096]{1,0:T(8,128)S(1)} %get-tuple-element.29), channel_id=1, source_target_pairs={{0,3},{1,0},{2,1},{3,2},{4,7},{5,4},{6,5},{7,6},{8,11},{9,8},{10,9... | collective-permute-start | bytes 1179656 | tf_op jit(solution)/shard_map/ppermute | solution.py:433
  14.7 12.8 %collective-permute-done.1.refs_2_ = f32[288,128]{1,0:T(8,128)S(1)} collective-permute-done((f32[288,128]{1,0:T(8,128)S(1)}, f32[288,128]{1,0:T(8,128)S(1)}, u32[]{:S(2)}, u32[]{:S(2)}) %collective-permute-start.1) | collective-permute-done | bytes 147488 | tf_op jit(solution)/shard_map/ppermute | solution.py:433
  27.4 0.0 collective-permute-done.2.refs_3_
  27.5 4.5 %collective-permute-start.3 = (f32[8,4096]{1,0:T(8,128)S(1)}, f32[8,4096]{1,0:T(8,128)S(1)}, u32[]{:S(2)}, u32[]{:S(2)}) collective-permute-start(f32[8,4096]{1,0:T(8,128)S(1)} %get-tuple-element.27), channel_id=1, source_target_pairs={{0,1},{1,2},{2,3},{3,0},{4,5},{5,6},{6,7},{7,4},{8,9},{9,10},{10,1... | collective-permute-start | bytes 393224 | tf_op jit(solution)/shard_map/ppermute | solution.py:433
  32.0 0.0 collective-permute-start.4
  32.0 9.9 %all-gather = f32[32,32,128]{2,1,0:T(8,128)S(1)} all-gather(f32[4,32,128]{2,1,0:T(8,128)S(1)} %pad_maximum_fusion), channel_id=2, replica_groups=mesh['blk'=8,'tm'=4] {'blk'}, dimensions={0}, use_global_device_ids=true | all-gather | bytes 589824 | tf_op jit(solution)/shard_map/all_gather | solution.py:447
  41.8 0.0 copy-done
  41.8 0.0 copy-done.1
  41.8 0.0 copy-done.2
  41.8 0.0 copy-done.3
  41.8 3.8 %lags_0.1 = (f32[32,8,4096]{2,1,0:T(8,128)}, f32[512,256]{1,0:T(8,128)S(1)}) custom-call(f32[32,4096]{1,0:T(8,128)S(1)} %get-tuple-element.20.refs_0_, f32[288,128]{1,0:T(8,128)S(1)} %collective-permute-done.refs_1_, f32[288,128]{1,0:T(8,128)S(1)} %collective-permute-done.1.refs_2_, f32[288,128]{1,0:T(8,128)S(1)} %collective-permute-done.2.refs_3_, ...), custom_call_target="tpu_custom_call" | custom-call | tf_op jit(solution)/shard_map/lags_0/pallas_call | solution.py:332
  45.7 0.0 collective-permute-done.6.refs_1_
  45.7 0.0 collective-permute-done.7.refs_2_
  45.7 0.0 collective-permute-done.5.refs_3_
  45.7 5.0 %lags_8.1.refs_9_ = f32[32,8,4096]{2,1,0:T(8,128)} custom-call(f32[32,4096]{1,0:T(8,128)S(1)} %get-tuple-element.20.refs_0_, f32[16,4096]{1,0:T(8,128)S(1)} %collective-permute-done.6.refs_1_, f32[16,4096]{1,0:T(8,128)S(1)} %collective-permute-done.7.refs_2_, f32[24,4096]{1,0:T(8,128)S(1)} %collective-permute-done.5.refs_3_, ...), custom_call_target="tpu_custom_call", output_to_operand_aliasing={{}: (9, {})} | custom-call | tf_op jit(solution)/shard_map/lags_8/pallas_call | solution.py:332
  50.8 0.0 collective-permute-done.3.refs_1_
  50.8 3.0 %collective-permute-done.4.refs_2_ = f32[8,4096]{1,0:T(8,128)S(1)} collective-permute-done((f32[8,4096]{1,0:T(8,128)S(1)}, f32[8,4096]{1,0:T(8,128)S(1)}, u32[]{:S(2)}, u32[]{:S(2)}) %collective-permute-start.4) | collective-permute-done | bytes 131104 | tf_op jit(solution)/shard_map/ppermute | solution.py:433
  53.7 2.9 %lags_24.1 = f32[32,8,4096]{2,1,0:T(8,128)} custom-call(f32[32,4096]{1,0:T(8,128)S(1)} %get-tuple-element.20.refs_0_, f32[8,4096]{1,0:T(8,128)S(1)} %collective-permute-done.3.refs_1_, f32[8,4096]{1,0:T(8,128)S(1)} %collective-permute-done.4.refs_2_, f32[24,4096]{1,0:T(8,128)S(1)} %collective-permute-done.5.refs_3_, ...), custom_call_target="tpu_custom_call", output_to_operand_aliasing={{}: (9, {})} | custom-call | tf_op jit(solution)/shard_map/lags_24/pallas_call | solution.py:332
  (4 shorter events, 0.0 us)
Async XLA Ops:
  0.0 41.8 %copy-start = (bf16[768,256]{1,0:T(8,128)(2,1)S(1)}, bf16[768,256]{1,0:T(8,128)(2,1)}, u32[]{:S(2)}) copy-start(bf16[768,256]{1,0:T(8,128)(2,1)} %constant.13.clone.refs_6_) | copy-start | bytes 1179652
  0.0 41.8 %copy-start.1 = (bf16[768,256]{1,0:T(8,128)(2,1)S(1)}, bf16[768,256]{1,0:T(8,128)(2,1)}, u32[]{:S(2)}) copy-start(bf16[768,256]{1,0:T(8,128)(2,1)} %constant.12.clone.refs_5_) | copy-start | bytes 1179652
  0.0 41.8 %copy-start.2 = (f32[34,128]{1,0:T(8,128)S(1)}, f32[34,128]{1,0:T(8,128)}, u32[]{:S(2)}) copy-start(f32[34,128]{1,0:T(8,128)} %constant.11.clone.refs_4_) | copy-start | bytes 52228
  0.0 41.8 %copy-start.3 = (f32[16,128]{1,0:T(8,128)S(1)}, f32[16,128]{1,0:T(8,128)}, u32[]{:S(2)}) copy-start(f32[16,128]{1,0:T(8,128)} %constant.14.clone.refs_7_) | copy-start | bytes 24580
  1.5 10.3 %collective-permute-start = (f32[288,128]{1,0:T(8,128)S(1)}, f32[288,128]{1,0:T(8,128)S(1)}, u32[]{:S(2)}, u32[]{:S(2)}) collective-permute-start(f32[288,128]{1,0:T(8,128)S(1)} %get-tuple-element.22), channel_id=1, source_target_pairs={{0,1},{1,2},{2,3},{3,0},{4,5},{5,6},{6,7},{7,4},{8,9},{9,10},{10,1... | collective-permute-start | bytes 442376 | tf_op jit(solution)/shard_map/ppermute | solution.py:433
  4.6 22.8 %collective-permute-start.1 = (f32[288,128]{1,0:T(8,128)S(1)}, f32[288,128]{1,0:T(8,128)S(1)}, u32[]{:S(2)}, u32[]{:S(2)}) collective-permute-start(f32[288,128]{1,0:T(8,128)S(1)} %get-tuple-element.23), channel_id=1, source_target_pairs={{0,2},{1,3},{2,0},{3,1},{4,6},{5,7},{6,4},{7,5},{8,10},{9,11},{10,... | collective-permute-start | bytes 442376 | tf_op jit(solution)/shard_map/ppermute | solution.py:433
  7.2 20.2 %collective-permute-start.2 = (f32[288,128]{1,0:T(8,128)S(1)}, f32[288,128]{1,0:T(8,128)S(1)}, u32[]{:S(2)}, u32[]{:S(2)}) collective-permute-start(f32[288,128]{1,0:T(8,128)S(1)} %get-tuple-element.24), channel_id=1, source_target_pairs={{0,3},{1,0},{2,1},{3,2},{4,7},{5,4},{6,5},{7,6},{8,11},{9,8},{10,9... | collective-permute-start | bytes 442376 | tf_op jit(solution)/shard_map/ppermute | solution.py:433
  10.8 34.9 %collective-permute-start.6 = (f32[16,4096]{1,0:T(8,128)S(1)}, f32[16,4096]{1,0:T(8,128)S(1)}, u32[]{:S(2)}, u32[]{:S(2)}) collective-permute-start(f32[16,4096]{1,0:T(8,128)S(1)} %get-tuple-element.32), channel_id=1, source_target_pairs={{0,1},{1,2},{2,3},{3,0},{4,5},{5,6},{6,7},{7,4},{8,9},{9,10},{10,1... | collective-permute-start | bytes 786440 | tf_op jit(solution)/shard_map/ppermute | solution.py:433
  11.5 34.2 %collective-permute-start.7 = (f32[16,4096]{1,0:T(8,128)S(1)}, f32[16,4096]{1,0:T(8,128)S(1)}, u32[]{:S(2)}, u32[]{:S(2)}) collective-permute-start(f32[16,4096]{1,0:T(8,128)S(1)} %get-tuple-element.33), channel_id=1, source_target_pairs={{0,2},{1,3},{2,0},{3,1},{4,6},{5,7},{6,4},{7,5},{8,10},{9,11},{10,... | collective-permute-start | bytes 786440 | tf_op jit(solution)/shard_map/ppermute | solution.py:433
  11.8 33.9 %collective-permute-start.5 = (f32[24,4096]{1,0:T(8,128)S(1)}, f32[24,4096]{1,0:T(8,128)S(1)}, u32[]{:S(2)}, u32[]{:S(2)}) collective-permute-start(f32[24,4096]{1,0:T(8,128)S(1)} %get-tuple-element.29), channel_id=1, source_target_pairs={{0,3},{1,0},{2,1},{3,2},{4,7},{5,4},{6,5},{7,6},{8,11},{9,8},{10,9... | collective-permute-start | bytes 1179656 | tf_op jit(solution)/shard_map/ppermute | solution.py:433
  27.5 23.3 %collective-permute-start.3 = (f32[8,4096]{1,0:T(8,128)S(1)}, f32[8,4096]{1,0:T(8,128)S(1)}, u32[]{:S(2)}, u32[]{:S(2)}) collective-permute-start(f32[8,4096]{1,0:T(8,128)S(1)} %get-tuple-element.27), channel_id=1, source_target_pairs={{0,1},{1,2},{2,3},{3,0},{4,5},{5,6},{6,7},{7,4},{8,9},{9,10},{10,1... | collective-permute-start | bytes 393224 | tf_op jit(solution)/shard_map/ppermute | solution.py:433
  32.0 21.7 %collective-permute-start.4 = (f32[8,4096]{1,0:T(8,128)S(1)}, f32[8,4096]{1,0:T(8,128)S(1)}, u32[]{:S(2)}, u32[]{:S(2)}) collective-permute-start(f32[8,4096]{1,0:T(8,128)S(1)} %get-tuple-element.28), channel_id=1, source_target_pairs={{0,2},{1,3},{2,0},{3,1},{4,6},{5,7},{6,4},{7,5},{8,10},{9,11},{10,... | collective-permute-start | bytes 393224 | tf_op jit(solution)/shard_map/ppermute | solution.py:433

commit v3 on v2

--- a/solution.py
+++ b/solution.py
@@ -433,20 +433,21 @@
         return lax.ppermute(array, "tm", pairs)
 
     steps = list(range(1, windows))
-    order = sorted(steps, key=lambda d: -min(d, windows - d))
+    order = sorted(steps, key=lambda d: (-min(d, windows - d), -d))
     *lead, row = tapered(records, gaps, mine, windows, steps, [])
     lead = dict(zip(steps, lead))
-    lead = {d: shift(lead[d], d) for d in order}
+    lead = {d: shift(lead[d], d) for d in [order[0], order[1], order[2]]}
     rows = jnp.stack([row] + [lead[d][:RADIX] for d in steps])
 
-    single, split = order[-1], order[:-1]
-    rest = [(d, SUB, cut - SUB) for d in split] + [(single, SUB, mine - SUB)] + [(d, cut, SUB) for d in split] + [(0, 0, mine)]
+    split = order
+    first = [order[0], order[1], order[2]]
+    rest = [(d, SUB, (cut if d in split else mine) - SUB) for d in first] + [(d, cut, SUB) for d in split] + [(0, 0, mine)]
     *bulk, own = tapered(records, gaps, mine, windows, [], rest)
     early, late = bulk[: len(steps)], bulk[len(steps) :]
-    rows, late = lax.optimization_barrier((rows, late))
     raw = lax.all_gather(rows, "blk", axis=0, tiled=False)
+    raw, late = lax.optimization_barrier((raw, late))
     raw = raw.reshape(-1, LANES)
-    early = {d: shift(array, d) for d, array in zip(order, early)}
+    early = {d: shift(array, d) for d, array in zip(first, early)}
     late = {d: shift(array, d) for d, array in zip(split, late)}
 
     tables = all_tables(1.0 / math.sqrt(NFFT * slots * windows))

time: 56.8 us -> 56.2 us (0.989)
  waiting for transfers between devices: 15.8 us -> 12.8 us
  starting transfers between devices: 15.4 us -> 18 us
    ppermute x8 -> x9, waiting for transfers between devices: 15.8 us -> 12.8 us  [shift(): return lax.ppermute(array, 'tm', pairs)]
    ppermute x8 -> x9, starting transfers between devices: 15.4 us -> 18 us  [shift(): return lax.ppermute(array, 'tm', pairs)]
  transfers between devices with their start and end apart: 8 -> 9, of which waited for: 2 -> 1; matrix products, arithmetic and copies ran while one was open for 0% -> 0% of each run, Pallas kernels for 20% -> 20%
where the time goes in v3:
time: 56.2 us; the launch traced here: 56 us
  starting transfers between devices  18 us (32%)
  Pallas kernels  15.5 us (28%)
  waiting for transfers between devices  12.8 us (23%)
  blocking collectives  9.62 us (17%)
    ppermute x9, starting transfers between devices, shift(): return lax.ppermute(array, 'tm', pairs)  18 us
    ppermute x9, waiting for transfers between devices, shift(): return lax.ppermute(array, 'tm', pairs)  12.8 us
    pallas_call x3, Pallas kernels, correlations(): pl.pallas_call(functools.partial(main_kernel, windows, batch, first, rows...  11.8 us
    all_gather x1, blocking collectives, shards(): raw = lax.all_gather(rows, 'blk', axis=0, tiled=False)  9.62 us
    pallas_call x2, Pallas kernels, tapered(): pl.pallas_call(functools.partial(taper_kernel, mine, windows, lead, rest)...  3.72 us
  transfers between devices with their start and end apart: 9, of which 1 were waited for; matrix products, arithmetic and copies ran while one was open for 0% of the time, Pallas kernels for 20%

profile of v3, /device:TPU:0, one launch (start us, length us, event | category | flops | bytes accessed | tf_op | source)
XLA Modules:
  0.0 56.0 jit_solution(7758409344517373884)
XLA Ops:
  0.0 0.0 copy-start
  0.0 0.0 copy-start.1
  0.0 0.0 copy-start.2
  0.0 0.0 copy-start.3
  0.0 1.5 %taper_lead.1 = (f32[288,128]{1,0:T(8,128)S(1)}, f32[288,128]{1,0:T(8,128)S(1)}, f32[288,128]{1,0:T(8,128)S(1)}, f32[32,128]{1,0:T(8,128)S(1)}) custom-call(s32[2,1,2]{2,1,0:T(1,128)} %gaps_hbm.3, f32[1,4096]{1,0:T(1,128)} %constant.10.clone.taper_hbm, f32[128,8192]{1,0:T(8,128)} %records_ref.3), custom_call_target="tpu_custom_call" | custom-call | tf_op jit(solution)/shard_map/taper_lead/pallas_call | solution.py:407
  1.5 3.1 %collective-permute-start = (f32[288,128]{1,0:T(8,128)S(1)}, f32[288,128]{1,0:T(8,128)S(1)}, u32[]{:S(2)}, u32[]{:S(2)}) collective-permute-start(f32[288,128]{1,0:T(8,128)S(1)} %get-tuple-element.24), channel_id=1, source_target_pairs={{0,1},{1,2},{2,3},{3,0},{4,5},{5,6},{6,7},{7,4},{8,9},{9,10},{10,1... | collective-permute-start | bytes 442376 | tf_op jit(solution)/shard_map/ppermute | solution.py:433
  4.6 2.6 %collective-permute-start.1 = (f32[288,128]{1,0:T(8,128)S(1)}, f32[288,128]{1,0:T(8,128)S(1)}, u32[]{:S(2)}, u32[]{:S(2)}) collective-permute-start(f32[288,128]{1,0:T(8,128)S(1)} %get-tuple-element.25), channel_id=1, source_target_pairs={{0,2},{1,3},{2,0},{3,1},{4,6},{5,7},{6,4},{7,5},{8,10},{9,11},{10,... | collective-permute-start | bytes 442376 | tf_op jit(solution)/shard_map/ppermute | solution.py:433
  7.2 1.3 %collective-permute-start.2 = (f32[288,128]{1,0:T(8,128)S(1)}, f32[288,128]{1,0:T(8,128)S(1)}, u32[]{:S(2)}, u32[]{:S(2)}) collective-permute-start(f32[288,128]{1,0:T(8,128)S(1)} %get-tuple-element.26), channel_id=1, source_target_pairs={{0,3},{1,0},{2,1},{3,2},{4,7},{5,4},{6,5},{7,6},{8,11},{9,8},{10,9... | collective-permute-start | bytes 442376 | tf_op jit(solution)/shard_map/ppermute | solution.py:433
  8.6 2.2 %taper.1 = (f32[16,4096]{1,0:T(8,128)S(1)}, f32[16,4096]{1,0:T(8,128)S(1)}, f32[16,4096]{1,0:T(8,128)S(1)}, f32[8,4096]{1,0:T(8,128)S(1)}, f32[8,4096]{1,0:T(8,1...) custom-call(s32[2,1,2]{2,1,0:T(1,128)} %gaps_hbm.3, f32[1,4096]{1,0:T(1,128)} %constant.10.clone.taper_hbm, ...), custom_call_target="tpu_custom_call" | custom-call | tf_op jit(solution)/shard_map/taper/pallas_call | solution.py:407
  10.8 0.7 %collective-permute-start.6 = (f32[16,4096]{1,0:T(8,128)S(1)}, f32[16,4096]{1,0:T(8,128)S(1)}, u32[]{:S(2)}, u32[]{:S(2)}) collective-permute-start(f32[16,4096]{1,0:T(8,128)S(1)} %get-tuple-element.35), channel_id=1, source_target_pairs={{0,1},{1,2},{2,3},{3,0},{4,5},{5,6},{6,7},{7,4},{8,9},{9,10},{10,1... | collective-permute-start | bytes 786440 | tf_op jit(solution)/shard_map/ppermute | solution.py:433
  11.5 0.3 collective-permute-start.7
  11.8 0.0 collective-permute-done.refs_1_
  11.8 2.8 %collective-permute-start.8 = (f32[16,4096]{1,0:T(8,128)S(1)}, f32[16,4096]{1,0:T(8,128)S(1)}, u32[]{:S(2)}, u32[]{:S(2)}) collective-permute-start(f32[16,4096]{1,0:T(8,128)S(1)} %get-tuple-element.37), channel_id=1, source_target_pairs={{0,3},{1,0},{2,1},{3,2},{4,7},{5,4},{6,5},{7,6},{8,11},{9,8},{10,9... | collective-permute-start | bytes 786440 | tf_op jit(solution)/shard_map/ppermute | solution.py:433
  14.7 12.8 %collective-permute-done.1.refs_2_ = f32[288,128]{1,0:T(8,128)S(1)} collective-permute-done((f32[288,128]{1,0:T(8,128)S(1)}, f32[288,128]{1,0:T(8,128)S(1)}, u32[]{:S(2)}, u32[]{:S(2)}) %collective-permute-start.1) | collective-permute-done | bytes 147488 | tf_op jit(solution)/shard_map/ppermute | solution.py:433
  27.4 0.0 collective-permute-done.2.refs_3_
  27.5 9.6 %all-gather = f32[32,32,128]{2,1,0:T(8,128)S(1)} all-gather(f32[4,32,128]{2,1,0:T(8,128)S(1)} %pad_maximum_fusion), channel_id=2, replica_groups=mesh['blk'=8,'tm'=4] {'blk'}, dimensions={0}, use_global_device_ids=true | all-gather | bytes 589824 | tf_op jit(solution)/shard_map/all_gather | solution.py:447
  37.1 4.7 %collective-permute-start.3 = (f32[8,4096]{1,0:T(8,128)S(1)}, f32[8,4096]{1,0:T(8,128)S(1)}, u32[]{:S(2)}, u32[]{:S(2)}) collective-permute-start(f32[8,4096]{1,0:T(8,128)S(1)} %get-tuple-element.30), channel_id=1, source_target_pairs={{0,1},{1,2},{2,3},{3,0},{4,5},{5,6},{6,7},{7,4},{8,9},{9,10},{10,1... | collective-permute-start | bytes 393224 | tf_op jit(solution)/shard_map/ppermute | solution.py:433
  41.8 0.0 collective-permute-start.4
  41.8 0.0 collective-permute-done.6.refs_1_
  41.8 2.4 %collective-permute-start.5 = (f32[8,4096]{1,0:T(8,128)S(1)}, f32[8,4096]{1,0:T(8,128)S(1)}, u32[]{:S(2)}, u32[]{:S(2)}) collective-permute-start(f32[8,4096]{1,0:T(8,128)S(1)} %get-tuple-element.32), channel_id=1, source_target_pairs={{0,3},{1,0},{2,1},{3,2},{4,7},{5,4},{6,5},{7,6},{8,11},{9,8},{10,9... | collective-permute-start | bytes 393224 | tf_op jit(solution)/shard_map/ppermute | solution.py:433
  44.2 0.0 copy-done
  44.2 0.0 copy-done.1
  44.2 0.0 copy-done.2
  44.2 0.0 copy-done.3
  44.2 3.8 %lags_0.1 = (f32[32,8,4096]{2,1,0:T(8,128)}, f32[512,256]{1,0:T(8,128)S(1)}) custom-call(f32[32,4096]{1,0:T(8,128)S(1)} %get-tuple-element.22.refs_0_, f32[288,128]{1,0:T(8,128)S(1)} %collective-permute-done.refs_1_, f32[288,128]{1,0:T(8,128)S(1)} %collective-permute-done.1.refs_2_, f32[288,128]{1,0:T(8,128)S(1)} %collective-permute-done.2.refs_3_, ...), custom_call_target="tpu_custom_call" | custom-call | tf_op jit(solution)/shard_map/lags_0/pallas_call | solution.py:332
  48.0 0.0 collective-permute-done.7.refs_2_
  48.0 0.0 collective-permute-done.8.refs_3_
  48.0 5.0 %lags_8.1.refs_9_ = f32[32,8,4096]{2,1,0:T(8,128)} custom-call(f32[32,4096]{1,0:T(8,128)S(1)} %get-tuple-element.22.refs_0_, f32[16,4096]{1,0:T(8,128)S(1)} %collective-permute-done.6.refs_1_, f32[16,4096]{1,0:T(8,128)S(1)} %collective-permute-done.7.refs_2_, f32[16,4096]{1,0:T(8,128)S(1)} %collective-permute-done.8.refs_3_, ...), custom_call_target="tpu_custom_call", output_to_operand_aliasing={{}: (9, {})} | custom-call | tf_op jit(solution)/shard_map/lags_8/pallas_call | solution.py:332
  53.1 0.0 collective-permute-done.3.refs_1_
  53.1 0.0 collective-permute-done.4.refs_2_
  53.1 0.0 collective-permute-done.5.refs_3_
  53.1 2.9 %lags_24.1 = f32[32,8,4096]{2,1,0:T(8,128)} custom-call(f32[32,4096]{1,0:T(8,128)S(1)} %get-tuple-element.22.refs_0_, f32[8,4096]{1,0:T(8,128)S(1)} %collective-permute-done.3.refs_1_, f32[8,4096]{1,0:T(8,128)S(1)} %collective-permute-done.4.refs_2_, f32[8,4096]{1,0:T(8,128)S(1)} %collective-permute-done.5.refs_3_, ...), custom_call_target="tpu_custom_call", output_to_operand_aliasing={{}: (9, {})} | custom-call | tf_op jit(solution)/shard_map/lags_24/pallas_call | solution.py:332
  (4 shorter events, 0.0 us)
Async XLA Ops:
  0.0 44.2 %copy-start = (bf16[768,256]{1,0:T(8,128)(2,1)S(1)}, bf16[768,256]{1,0:T(8,128)(2,1)}, u32[]{:S(2)}) copy-start(bf16[768,256]{1,0:T(8,128)(2,1)} %constant.13.clone.refs_6_) | copy-start | bytes 1179652
  0.0 44.2 %copy-start.1 = (bf16[768,256]{1,0:T(8,128)(2,1)S(1)}, bf16[768,256]{1,0:T(8,128)(2,1)}, u32[]{:S(2)}) copy-start(bf16[768,256]{1,0:T(8,128)(2,1)} %constant.12.clone.refs_5_) | copy-start | bytes 1179652
  0.0 44.2 %copy-start.2 = (f32[34,128]{1,0:T(8,128)S(1)}, f32[34,128]{1,0:T(8,128)}, u32[]{:S(2)}) copy-start(f32[34,128]{1,0:T(8,128)} %constant.11.clone.refs_4_) | copy-start | bytes 52228
  0.0 44.2 %copy-start.3 = (f32[16,128]{1,0:T(8,128)S(1)}, f32[16,128]{1,0:T(8,128)}, u32[]{:S(2)}) copy-start(f32[16,128]{1,0:T(8,128)} %constant.14.clone.refs_7_) | copy-start | bytes 24580
  1.5 10.3 %collective-permute-start = (f32[288,128]{1,0:T(8,128)S(1)}, f32[288,128]{1,0:T(8,128)S(1)}, u32[]{:S(2)}, u32[]{:S(2)}) collective-permute-start(f32[288,128]{1,0:T(8,128)S(1)} %get-tuple-element.24), channel_id=1, source_target_pairs={{0,1},{1,2},{2,3},{3,0},{4,5},{5,6},{6,7},{7,4},{8,9},{9,10},{10,1... | collective-permute-start | bytes 442376 | tf_op jit(solution)/shard_map/ppermute | solution.py:433
  4.6 22.8 %collective-permute-start.1 = (f32[288,128]{1,0:T(8,128)S(1)}, f32[288,128]{1,0:T(8,128)S(1)}, u32[]{:S(2)}, u32[]{:S(2)}) collective-permute-start(f32[288,128]{1,0:T(8,128)S(1)} %get-tuple-element.25), channel_id=1, source_target_pairs={{0,2},{1,3},{2,0},{3,1},{4,6},{5,7},{6,4},{7,5},{8,10},{9,11},{10,... | collective-permute-start | bytes 442376 | tf_op jit(solution)/shard_map/ppermute | solution.py:433
  7.2 20.2 %collective-permute-start.2 = (f32[288,128]{1,0:T(8,128)S(1)}, f32[288,128]{1,0:T(8,128)S(1)}, u32[]{:S(2)}, u32[]{:S(2)}) collective-permute-start(f32[288,128]{1,0:T(8,128)S(1)} %get-tuple-element.26), channel_id=1, source_target_pairs={{0,3},{1,0},{2,1},{3,2},{4,7},{5,4},{6,5},{7,6},{8,11},{9,8},{10,9... | collective-permute-start | bytes 442376 | tf_op jit(solution)/shard_map/ppermute | solution.py:433
  10.8 31.0 %collective-permute-start.6 = (f32[16,4096]{1,0:T(8,128)S(1)}, f32[16,4096]{1,0:T(8,128)S(1)}, u32[]{:S(2)}, u32[]{:S(2)}) collective-permute-start(f32[16,4096]{1,0:T(8,128)S(1)} %get-tuple-element.35), channel_id=1, source_target_pairs={{0,1},{1,2},{2,3},{3,0},{4,5},{5,6},{6,7},{7,4},{8,9},{9,10},{10,1... | collective-permute-start | bytes 786440 | tf_op jit(solution)/shard_map/ppermute | solution.py:433
  11.5 36.5 %collective-permute-start.7 = (f32[16,4096]{1,0:T(8,128)S(1)}, f32[16,4096]{1,0:T(8,128)S(1)}, u32[]{:S(2)}, u32[]{:S(2)}) collective-permute-start(f32[16,4096]{1,0:T(8,128)S(1)} %get-tuple-element.36), channel_id=1, source_target_pairs={{0,2},{1,3},{2,0},{3,1},{4,6},{5,7},{6,4},{7,5},{8,10},{9,11},{10,... | collective-permute-start | bytes 786440 | tf_op jit(solution)/shard_map/ppermute | solution.py:433
  11.8 36.2 %collective-permute-start.8 = (f32[16,4096]{1,0:T(8,128)S(1)}, f32[16,4096]{1,0:T(8,128)S(1)}, u32[]{:S(2)}, u32[]{:S(2)}) collective-permute-start(f32[16,4096]{1,0:T(8,128)S(1)} %get-tuple-element.37), channel_id=1, source_target_pairs={{0,3},{1,0},{2,1},{3,2},{4,7},{5,4},{6,5},{7,6},{8,11},{9,8},{10,9... | collective-permute-start | bytes 786440 | tf_op jit(solution)/shard_map/ppermute | solution.py:433
  37.1 16.0 %collective-permute-start.3 = (f32[8,4096]{1,0:T(8,128)S(1)}, f32[8,4096]{1,0:T(8,128)S(1)}, u32[]{:S(2)}, u32[]{:S(2)}) collective-permute-start(f32[8,4096]{1,0:T(8,128)S(1)} %get-tuple-element.30), channel_id=1, source_target_pairs={{0,1},{1,2},{2,3},{3,0},{4,5},{5,6},{6,7},{7,4},{8,9},{9,10},{10,1... | collective-permute-start | bytes 393224 | tf_op jit(solution)/shard_map/ppermute | solution.py:433
  41.8 11.3 %collective-permute-start.4 = (f32[8,4096]{1,0:T(8,128)S(1)}, f32[8,4096]{1,0:T(8,128)S(1)}, u32[]{:S(2)}, u32[]{:S(2)}) collective-permute-start(f32[8,4096]{1,0:T(8,128)S(1)} %get-tuple-element.31), channel_id=1, source_target_pairs={{0,2},{1,3},{2,0},{3,1},{4,6},{5,7},{6,4},{7,5},{8,10},{9,11},{10,... | collective-permute-start | bytes 393224 | tf_op jit(solution)/shard_map/ppermute | solution.py:433
  41.8 11.3 %collective-permute-start.5 = (f32[8,4096]{1,0:T(8,128)S(1)}, f32[8,4096]{1,0:T(8,128)S(1)}, u32[]{:S(2)}, u32[]{:S(2)}) collective-permute-start(f32[8,4096]{1,0:T(8,128)S(1)} %get-tuple-element.32), channel_id=1, source_target_pairs={{0,3},{1,0},{2,1},{3,2},{4,7},{5,4},{6,5},{7,6},{8,11},{9,8},{10,9... | collective-permute-start | bytes 393224 | tf_op jit(solution)/shard_map/ppermute | solution.py:433

commit v4 on v3

--- a/solution.py
+++ b/solution.py
@@ -156,7 +156,7 @@
         power = power + (r * r + i * i)
     power = power + pltpu.roll(power, QUART, 1)
     power = power + pltpu.roll(power, QUART // 2, 1)
-    scale = 1.0 / jnp.sqrt(power * (1.0 / BAND) + EPS)
+    scale = lax.rsqrt(power * (1.0 / BAND) + EPS)
     return [r * scale for r in re], [i * scale for i in im]
 
 
@@ -443,17 +443,19 @@
     first = [order[0], order[1], order[2]]
     rest = [(d, SUB, (cut if d in split else mine) - SUB) for d in first] + [(d, cut, SUB) for d in split] + [(0, 0, mine)]
     *bulk, own = tapered(records, gaps, mine, windows, [], rest)
-    early, late = bulk[: len(steps)], bulk[len(steps) :]
+    early, late = list(bulk[: len(steps)]), bulk[len(steps) :]
+    rows, held = lax.optimization_barrier((rows, early[0]))
+    early[0] = held
     raw = lax.all_gather(rows, "blk", axis=0, tiled=False)
-    raw, late = lax.optimization_barrier((raw, late))
     raw = raw.reshape(-1, LANES)
     early = {d: shift(array, d) for d, array in zip(first, early)}
-    late = {d: shift(array, d) for d, array in zip(split, late)}
 
     tables = all_tables(1.0 / math.sqrt(NFFT * slots * windows))
     pieces = [(own, 0)] + [(lead[d], None) for d in steps]
     more = [(own, SUB)] + [(early[d], 0) for d in steps]
     out, source = correlations(pieces, tables, mine, 0, SUB, raw=raw)
+    source, late = lax.optimization_barrier((source, late))
+    late = {d: shift(array, d) for d, array in zip(split, late)}
     (out,) = correlations(more, tables, mine, SUB, cut - SUB, source=source, before=out)
     pieces = [(own, cut)] + [(late[d], 0) if d in late else (early[d], cut - SUB) for d in steps]
     return correlations(pieces, tables, mine, cut, SUB, source=source, before=out)[0]

time: 56.2 us -> 55.9 us (level)
  starting transfers between devices: 18 us -> 16 us
  waiting for transfers between devices: 12.8 us -> 14.3 us
    ppermute x9, starting transfers between devices: 18 us -> 16 us  [shift(): return lax.ppermute(array, 'tm', pairs)]
    ppermute x9, waiting for transfers between devices: 12.8 us -> 14.3 us  [shift(): return lax.ppermute(array, 'tm', pairs)]
  transfers between devices with their start and end apart: 9 -> 9, of which waited for: 1 -> 2; matrix products, arithmetic and copies ran while one was open for 0% -> 0% of each run, Pallas kernels for 20% -> 20%
where the time goes in v4:
time: 55.9 us; the launch traced here: 55.6 us
  starting transfers between devices  16 us (29%)
  Pallas kernels  15.4 us (28%)
  waiting for transfers between devices  14.3 us (26%)
  blocking collectives  9.87 us (18%)
    ppermute x9, starting transfers between devices, shift(): return lax.ppermute(array, 'tm', pairs)  16 us
    ppermute x9, waiting for transfers between devices, shift(): return lax.ppermute(array, 'tm', pairs)  14.3 us
    pallas_call x3, Pallas kernels, correlations(): pl.pallas_call(functools.partial(main_kernel, windows, batch, first, rows...  11.6 us
    all_gather x1, blocking collectives, shards(): raw = lax.all_gather(rows, 'blk', axis=0, tiled=False)  9.87 us
    pallas_call x2, Pallas kernels, tapered(): pl.pallas_call(functools.partial(taper_kernel, mine, windows, lead, rest)...  3.72 us
  transfers between devices with their start and end apart: 9, of which 2 were waited for; matrix products, arithmetic and copies ran while one was open for 0% of the time, Pallas kernels for 20%

profile of v4, /device:TPU:0, one launch (start us, length us, event | category | flops | bytes accessed | tf_op | source)
XLA Modules:
  0.0 55.6 jit_solution(18205944117115935832)
XLA Ops:
  0.0 0.0 copy-start
  0.0 0.0 copy-start.1
  0.0 0.0 copy-start.2
  0.0 0.0 copy-start.3
  0.0 1.5 %taper_lead.1 = (f32[288,128]{1,0:T(8,128)S(1)}, f32[288,128]{1,0:T(8,128)S(1)}, f32[288,128]{1,0:T(8,128)S(1)}, f32[32,128]{1,0:T(8,128)S(1)}) custom-call(s32[2,1,2]{2,1,0:T(1,128)} %gaps_hbm.3, f32[1,4096]{1,0:T(1,128)} %constant.10.clone.taper_hbm, f32[128,8192]{1,0:T(8,128)} %records_ref.3), custom_call_target="tpu_custom_call" | custom-call | tf_op jit(solution)/shard_map/taper_lead/pallas_call | solution.py:407
  1.5 5.1 %collective-permute-start.2 = (f32[288,128]{1,0:T(8,128)S(1)}, f32[288,128]{1,0:T(8,128)S(1)}, u32[]{:S(2)}, u32[]{:S(2)}) collective-permute-start(f32[288,128]{1,0:T(8,128)S(1)} %get-tuple-element.27), channel_id=1, source_target_pairs={{0,3},{1,0},{2,1},{3,2},{4,7},{5,4},{6,5},{7,6},{8,11},{9,8},{10,9... | collective-permute-start | bytes 442376 | tf_op jit(solution)/shard_map/ppermute | solution.py:433
  6.6 0.0 collective-permute-start
  6.6 1.0 %collective-permute-start.1 = (f32[288,128]{1,0:T(8,128)S(1)}, f32[288,128]{1,0:T(8,128)S(1)}, u32[]{:S(2)}, u32[]{:S(2)}) collective-permute-start(f32[288,128]{1,0:T(8,128)S(1)} %get-tuple-element.26), channel_id=1, source_target_pairs={{0,2},{1,3},{2,0},{3,1},{4,6},{5,7},{6,4},{7,5},{8,10},{9,11},{10,... | collective-permute-start | bytes 442376 | tf_op jit(solution)/shard_map/ppermute | solution.py:433
  7.7 2.2 %taper.1 = (f32[16,4096]{1,0:T(8,128)S(1)}, f32[16,4096]{1,0:T(8,128)S(1)}, f32[16,4096]{1,0:T(8,128)S(1)}, f32[8,4096]{1,0:T(8,128)S(1)}, f32[8,4096]{1,0:T(8,1...) custom-call(s32[2,1,2]{2,1,0:T(1,128)} %gaps_hbm.3, f32[1,4096]{1,0:T(1,128)} %constant.10.clone.taper_hbm, ...), custom_call_target="tpu_custom_call" | custom-call | tf_op jit(solution)/shard_map/taper/pallas_call | solution.py:407
  9.9 3.4 %collective-permute-start.6 = (f32[16,4096]{1,0:T(8,128)S(1)}, f32[16,4096]{1,0:T(8,128)S(1)}, u32[]{:S(2)}, u32[]{:S(2)}) collective-permute-start(f32[16,4096]{1,0:T(8,128)S(1)} %get-tuple-element.39), channel_id=1, source_target_pairs={{0,1},{1,2},{2,3},{3,0},{4,5},{5,6},{6,7},{7,4},{8,9},{9,10},{10,1... | collective-permute-start | bytes 786440 | tf_op jit(solution)/shard_map/ppermute | solution.py:433
  13.3 0.4 collective-permute-start.8
  13.8 0.0 collective-permute-done.2.refs_3_
  13.8 12.2 %collective-permute-done.1.refs_2_ = f32[288,128]{1,0:T(8,128)S(1)} collective-permute-done((f32[288,128]{1,0:T(8,128)S(1)}, f32[288,128]{1,0:T(8,128)S(1)}, u32[]{:S(2)}, u32[]{:S(2)}) %collective-permute-start.1) | collective-permute-done | bytes 147488 | tf_op jit(solution)/shard_map/ppermute | solution.py:433
  26.0 0.0 collective-permute-done.refs_1_
  26.0 0.1 collective-permute-start.7
  26.1 9.9 %all-gather = f32[32,32,128]{2,1,0:T(8,128)S(1)} all-gather(f32[4,32,128]{2,1,0:T(8,128)S(1)} %pad_maximum_fusion), channel_id=2, replica_groups=mesh['blk'=8,'tm'=4] {'blk'}, dimensions={0}, use_global_device_ids=true | all-gather | bytes 589824 | tf_op jit(solution)/shard_map/all_gather | solution.py:449
  35.9 0.0 copy-done
  35.9 0.0 copy-done.1
  35.9 0.0 copy-done.2
  35.9 0.0 copy-done.3
  35.9 3.8 %lags_0.1 = (f32[32,8,4096]{2,1,0:T(8,128)}, f32[512,256]{1,0:T(8,128)S(1)}) custom-call(f32[32,4096]{1,0:T(8,128)S(1)} %get-tuple-element.24.refs_0_, f32[288,128]{1,0:T(8,128)S(1)} %collective-permute-done.refs_1_, f32[288,128]{1,0:T(8,128)S(1)} %collective-permute-done.1.refs_2_, f32[288,128]{1,0:T(8,128)S(1)} %collective-permute-done.2.refs_3_, ...), custom_call_target="tpu_custom_call" | custom-call | tf_op jit(solution)/shard_map/lags_0/pallas_call | solution.py:332
  39.8 0.1 collective-permute-start.3
  39.8 3.0 %collective-permute-start.4 = (f32[8,4096]{1,0:T(8,128)S(1)}, f32[8,4096]{1,0:T(8,128)S(1)}, u32[]{:S(2)}, u32[]{:S(2)}) collective-permute-start(f32[8,4096]{1,0:T(8,128)S(1)} %get-tuple-element.36), channel_id=1, source_target_pairs={{0,2},{1,3},{2,0},{3,1},{4,6},{5,7},{6,4},{7,5},{8,10},{9,11},{10,... | collective-permute-start | bytes 393224 | tf_op jit(solution)/shard_map/ppermute | solution.py:433
  42.8 0.0 collective-permute-done.6.refs_1_
  42.8 2.8 %collective-permute-start.5 = (f32[8,4096]{1,0:T(8,128)S(1)}, f32[8,4096]{1,0:T(8,128)S(1)}, u32[]{:S(2)}, u32[]{:S(2)}) collective-permute-start(f32[8,4096]{1,0:T(8,128)S(1)} %get-tuple-element.37), channel_id=1, source_target_pairs={{0,3},{1,0},{2,1},{3,2},{4,7},{5,4},{6,5},{7,6},{8,11},{9,8},{10,9... | collective-permute-start | bytes 393224 | tf_op jit(solution)/shard_map/ppermute | solution.py:433
  45.7 0.0 collective-permute-done.8.refs_3_
  45.7 0.0 collective-permute-done.7.refs_2_
  45.7 5.0 %lags_8.1.refs_9_ = f32[32,8,4096]{2,1,0:T(8,128)} custom-call(f32[32,4096]{1,0:T(8,128)S(1)} %get-tuple-element.24.refs_0_, f32[16,4096]{1,0:T(8,128)S(1)} %collective-permute-done.6.refs_1_, f32[16,4096]{1,0:T(8,128)S(1)} %collective-permute-done.7.refs_2_, f32[16,4096]{1,0:T(8,128)S(1)} %collective-permute-done.8.refs_3_, ...), custom_call_target="tpu_custom_call", output_to_operand_aliasing={{}: (9, {})} | custom-call | tf_op jit(solution)/shard_map/lags_8/pallas_call | solution.py:332
  50.6 0.0 collective-permute-done.3.refs_1_
  50.6 2.1 %collective-permute-done.4.refs_2_ = f32[8,4096]{1,0:T(8,128)S(1)} collective-permute-done((f32[8,4096]{1,0:T(8,128)S(1)}, f32[8,4096]{1,0:T(8,128)S(1)}, u32[]{:S(2)}, u32[]{:S(2)}) %collective-permute-start.4) | collective-permute-done | bytes 131104 | tf_op jit(solution)/shard_map/ppermute | solution.py:433
  52.7 0.0 collective-permute-done.5.refs_3_
  52.7 2.9 %lags_24.1 = f32[32,8,4096]{2,1,0:T(8,128)} custom-call(f32[32,4096]{1,0:T(8,128)S(1)} %get-tuple-element.24.refs_0_, f32[8,4096]{1,0:T(8,128)S(1)} %collective-permute-done.3.refs_1_, f32[8,4096]{1,0:T(8,128)S(1)} %collective-permute-done.4.refs_2_, f32[8,4096]{1,0:T(8,128)S(1)} %collective-permute-done.5.refs_3_, ...), custom_call_target="tpu_custom_call", output_to_operand_aliasing={{}: (9, {})} | custom-call | tf_op jit(solution)/shard_map/lags_24/pallas_call | solution.py:332
  (4 shorter events, 0.0 us)
Async XLA Ops:
  0.0 35.9 %copy-start = (bf16[768,256]{1,0:T(8,128)(2,1)S(1)}, bf16[768,256]{1,0:T(8,128)(2,1)}, u32[]{:S(2)}) copy-start(bf16[768,256]{1,0:T(8,128)(2,1)} %constant.12.clone.refs_5_) | copy-start | bytes 1179652
  0.0 35.9 %copy-start.1 = (bf16[768,256]{1,0:T(8,128)(2,1)S(1)}, bf16[768,256]{1,0:T(8,128)(2,1)}, u32[]{:S(2)}) copy-start(bf16[768,256]{1,0:T(8,128)(2,1)} %constant.13.clone.refs_6_) | copy-start | bytes 1179652
  0.0 35.9 %copy-start.2 = (f32[34,128]{1,0:T(8,128)S(1)}, f32[34,128]{1,0:T(8,128)}, u32[]{:S(2)}) copy-start(f32[34,128]{1,0:T(8,128)} %constant.11.clone.refs_4_) | copy-start | bytes 52228
  0.0 35.9 %copy-start.3 = (f32[16,128]{1,0:T(8,128)S(1)}, f32[16,128]{1,0:T(8,128)}, u32[]{:S(2)}) copy-start(f32[16,128]{1,0:T(8,128)} %constant.14.clone.refs_7_) | copy-start | bytes 24580
  1.5 12.2 %collective-permute-start.2 = (f32[288,128]{1,0:T(8,128)S(1)}, f32[288,128]{1,0:T(8,128)S(1)}, u32[]{:S(2)}, u32[]{:S(2)}) collective-permute-start(f32[288,128]{1,0:T(8,128)S(1)} %get-tuple-element.27), channel_id=1, source_target_pairs={{0,3},{1,0},{2,1},{3,2},{4,7},{5,4},{6,5},{7,6},{8,11},{9,8},{10,9... | collective-permute-start | bytes 442376 | tf_op jit(solution)/shard_map/ppermute | solution.py:433
  6.6 19.3 %collective-permute-start = (f32[288,128]{1,0:T(8,128)S(1)}, f32[288,128]{1,0:T(8,128)S(1)}, u32[]{:S(2)}, u32[]{:S(2)}) collective-permute-start(f32[288,128]{1,0:T(8,128)S(1)} %get-tuple-element.25), channel_id=1, source_target_pairs={{0,1},{1,2},{2,3},{3,0},{4,5},{5,6},{6,7},{7,4},{8,9},{9,10},{10,1... | collective-permute-start | bytes 442376 | tf_op jit(solution)/shard_map/ppermute | solution.py:433
  6.6 19.3 %collective-permute-start.1 = (f32[288,128]{1,0:T(8,128)S(1)}, f32[288,128]{1,0:T(8,128)S(1)}, u32[]{:S(2)}, u32[]{:S(2)}) collective-permute-start(f32[288,128]{1,0:T(8,128)S(1)} %get-tuple-element.26), channel_id=1, source_target_pairs={{0,2},{1,3},{2,0},{3,1},{4,6},{5,7},{6,4},{7,5},{8,10},{9,11},{10,... | collective-permute-start | bytes 442376 | tf_op jit(solution)/shard_map/ppermute | solution.py:433
  9.9 32.9 %collective-permute-start.6 = (f32[16,4096]{1,0:T(8,128)S(1)}, f32[16,4096]{1,0:T(8,128)S(1)}, u32[]{:S(2)}, u32[]{:S(2)}) collective-permute-start(f32[16,4096]{1,0:T(8,128)S(1)} %get-tuple-element.39), channel_id=1, source_target_pairs={{0,1},{1,2},{2,3},{3,0},{4,5},{5,6},{6,7},{7,4},{8,9},{9,10},{10,1... | collective-permute-start | bytes 786440 | tf_op jit(solution)/shard_map/ppermute | solution.py:433
  13.3 32.4 %collective-permute-start.8 = (f32[16,4096]{1,0:T(8,128)S(1)}, f32[16,4096]{1,0:T(8,128)S(1)}, u32[]{:S(2)}, u32[]{:S(2)}) collective-permute-start(f32[16,4096]{1,0:T(8,128)S(1)} %get-tuple-element.41), channel_id=1, source_target_pairs={{0,3},{1,0},{2,1},{3,2},{4,7},{5,4},{6,5},{7,6},{8,11},{9,8},{10,9... | collective-permute-start | bytes 786440 | tf_op jit(solution)/shard_map/ppermute | solution.py:433
  26.0 19.7 %collective-permute-start.7 = (f32[16,4096]{1,0:T(8,128)S(1)}, f32[16,4096]{1,0:T(8,128)S(1)}, u32[]{:S(2)}, u32[]{:S(2)}) collective-permute-start(f32[16,4096]{1,0:T(8,128)S(1)} %get-tuple-element.40), channel_id=1, source_target_pairs={{0,2},{1,3},{2,0},{3,1},{4,6},{5,7},{6,4},{7,5},{8,10},{9,11},{10,... | collective-permute-start | bytes 786440 | tf_op jit(solution)/shard_map/ppermute | solution.py:433
  39.8 10.9 %collective-permute-start.3 = (f32[8,4096]{1,0:T(8,128)S(1)}, f32[8,4096]{1,0:T(8,128)S(1)}, u32[]{:S(2)}, u32[]{:S(2)}) collective-permute-start(f32[8,4096]{1,0:T(8,128)S(1)} %get-tuple-element.35), channel_id=1, source_target_pairs={{0,1},{1,2},{2,3},{3,0},{4,5},{5,6},{6,7},{7,4},{8,9},{9,10},{10,1... | collective-permute-start | bytes 393224 | tf_op jit(solution)/shard_map/ppermute | solution.py:433
  39.8 12.9 %collective-permute-start.4 = (f32[8,4096]{1,0:T(8,128)S(1)}, f32[8,4096]{1,0:T(8,128)S(1)}, u32[]{:S(2)}, u32[]{:S(2)}) collective-permute-start(f32[8,4096]{1,0:T(8,128)S(1)} %get-tuple-element.36), channel_id=1, source_target_pairs={{0,2},{1,3},{2,0},{3,1},{4,6},{5,7},{6,4},{7,5},{8,10},{9,11},{10,... | collective-permute-start | bytes 393224 | tf_op jit(solution)/shard_map/ppermute | solution.py:433
  42.8 9.9 %collective-permute-start.5 = (f32[8,4096]{1,0:T(8,128)S(1)}, f32[8,4096]{1,0:T(8,128)S(1)}, u32[]{:S(2)}, u32[]{:S(2)}) collective-permute-start(f32[8,4096]{1,0:T(8,128)S(1)} %get-tuple-element.37), channel_id=1, source_target_pairs={{0,3},{1,0},{2,1},{3,2},{4,7},{5,4},{6,5},{7,6},{8,11},{9,8},{10,9... | collective-permute-start | bytes 393224 | tf_op jit(solution)/shard_map/ppermute | solution.py:433
